TPU v7x, 256 devices: a whole 4x4x8 slice. The times are simulated.
256 devices in a mesh: ctx: 16 (over x, z_hi, core), head: 16 (over z_lo, y).
Axes of the slice: x: 4, y: 4, z: 8 (z_hi: 2, z_lo: 4; z = z_hi * 4 + z_lo), core: 2. Of those that a mesh axis runs over, the one named last changes fastest.
Arguments:
- queries: bfloat16 [36864, 2048], P(('ctx', 'head')), may hold values from -8 to 8
- keys: bfloat16 [36864, 2048], P(('ctx', 'head')), may hold values from -8 to 8
- values: bfloat16 [36864, 2048], P(('ctx', 'head')), may hold values from -6 to 6
- out_grad: bfloat16 [36864, 2048], P(('ctx', 'head')), may hold values from -6 to 6
- key_tiles: int32 [16, 192, 9], P('head', 'ctx'), may hold values from -1 to 191, as said below
Outputs:
- attention_out: bfloat16 [36864, 2048], P(('ctx', 'head'))
- query_grad: bfloat16 [36864, 2048], P(('ctx', 'head'))
- key_grad: bfloat16 [36864, 2048], P(('ctx', 'head'))
- value_grad: bfloat16 [36864, 2048], P(('ctx', 'head'))
Inputs may be any that keep to these rules, and one draw needn't show every extreme that they name: `key_tiles`: row (h, i) lists in ascending order, then -1 to fill 9 places, the tiles of a grid of 8 time slabs of 3 by 8 tiles (tile i in slab i // 24, tile row (i % 24) // 8, tile column i % 8) that differ from tile i by at most one along tile columns and along one more direction fixed for each head, time or tile rows, and not at all along the third. Both kinds of head occur, and some rows are full.
All inputs are finite; a program needn't handle non-finite values.
Results may differ from a plain program's by a relative error of at most 0.02.
Values may be sent and summed in bfloat16 or wider, within the bound.
A program may use at most 128 MiB of HBM per device.

v0:
```python
import math

import jax
import jax.numpy as jnp
from jax import lax
from jax.sharding import PartitionSpec as P

DH = 128
TILE = 192
GROUP_TILES = 12
REACH = 3


NEG_FILL = -1e30


def shifted(array, axis, by):
    devices = lax.axis_size(axis)
    pairs = [(i, i + by) for i in range(devices) if 0 <= i + by < devices]
    return lax.ppermute(array, axis, pairs)


def tile_block(query_rows, grad_rows, key_rows, value_rows, present, score_scale):
    scores = (
        jnp.einsum("aqd,akjd->aqkj", query_rows, key_rows, preferred_element_type=jnp.float32)
        * score_scale
    )
    scores = jnp.where(present[:, None, :, None], scores, NEG_FILL)
    row_top = jnp.max(scores, axis=(2, 3), keepdims=True)
    raised = jnp.exp(scores - row_top)
    weights = (raised / jnp.sum(raised, axis=(2, 3), keepdims=True)).astype(jnp.bfloat16)
    attended = jnp.einsum(
        "aqkj,akjd->aqd", weights, value_rows, preferred_element_type=jnp.float32
    ).astype(jnp.bfloat16)
    row_delta = jnp.sum(grad_rows.astype(jnp.float32) * attended.astype(jnp.float32), axis=2)[
        :, :, None, None
    ]
    weight_grad = jnp.einsum(
        "aqd,akjd->aqkj", grad_rows, value_rows, preferred_element_type=jnp.float32
    )
    score_grad = (weights.astype(jnp.float32) * (weight_grad - row_delta) * score_scale).astype(
        jnp.bfloat16
    )
    query_grad = jnp.einsum(
        "aqkj,akjd->aqd", score_grad, key_rows, preferred_element_type=jnp.float32
    ).astype(jnp.bfloat16)
    key_part = jnp.einsum(
        "aqkj,aqd->akjd", score_grad, query_rows, preferred_element_type=jnp.float32
    )
    value_part = jnp.einsum(
        "aqkj,aqd->akjd", weights, grad_rows, preferred_element_type=jnp.float32
    )
    return (attended, query_grad, key_part, value_part)


def per_device(queries, keys, values, out_grad, key_tiles):
    score_scale = 1.0 / math.sqrt(DH)
    head_queries, head_keys, head_values, head_grads = (
        lax.all_to_all(queries, "head", split_axis=1, concat_axis=0, tiled=True),
        lax.all_to_all(keys, "head", split_axis=1, concat_axis=0, tiled=True),
        lax.all_to_all(values, "head", split_axis=1, concat_axis=0, tiled=True),
        lax.all_to_all(out_grad, "head", split_axis=1, concat_axis=0, tiled=True),
    )
    group_rows = head_queries.shape[0]
    own_block = jnp.stack([head_keys, head_values], axis=1)
    ctx_index = lax.axis_index("ctx")
    slot_count = 2 * REACH + 1
    kept = []
    for slot_index in range(slot_count):
        offset = slot_index - REACH
        if offset == 0:
            kept.append(own_block)
        else:
            kept.append(shifted(own_block, "ctx", -offset))
    nearby = jnp.stack(kept)
    tile_store = nearby.reshape(slot_count * GROUP_TILES, TILE, 2, DH)
    own_lists = key_tiles[0]
    present_all = own_lists >= 0
    local_tiles = jnp.where(present_all, own_lists - (ctx_index - REACH) * GROUP_TILES, 0)
    query_tiles = head_queries.reshape(GROUP_TILES, TILE, DH)
    grad_tiles = head_grads.reshape(GROUP_TILES, TILE, DH)

    def advance(grad_store, block_index):
        first_tile = block_index * 4
        query_rows = lax.dynamic_slice_in_dim(query_tiles, first_tile, 4, 0)
        grad_rows = lax.dynamic_slice_in_dim(grad_tiles, first_tile, 4, 0)
        chosen = lax.dynamic_slice_in_dim(local_tiles, first_tile, 4, 0)
        present = lax.dynamic_slice_in_dim(present_all, first_tile, 4, 0)
        gathered = tile_store[chosen]
        attended, query_grad, key_part, value_part = tile_block(
            query_rows, grad_rows, gathered[:, :, :, 0], gathered[:, :, :, 1], present, score_scale
        )
        both_parts = jnp.stack([key_part, value_part], axis=3).reshape(-1, TILE, 2, DH)
        grad_store = grad_store.at[chosen.reshape(-1)].add(both_parts)
        return (grad_store, (attended, query_grad))

    zero_store = jnp.zeros((slot_count * GROUP_TILES, TILE, 2, DH), jnp.float32)
    grad_store, produced = lax.scan(
        advance, zero_store, jnp.arange(GROUP_TILES // 4, dtype=jnp.int32)
    )
    rounded = grad_store.astype(jnp.bfloat16).reshape(slot_count, group_rows, 2, DH)
    total = rounded[REACH].astype(jnp.float32)
    for slot_index in range(slot_count):
        offset = slot_index - REACH
        if offset != 0:
            arrived = shifted(rounded[slot_index], "ctx", offset)
            total = total + arrived.astype(jnp.float32)
    key_grad = total[:, 0].astype(jnp.bfloat16)
    value_grad = total[:, 1].astype(jnp.bfloat16)
    attended = produced[0].reshape(group_rows, DH)
    query_grad = produced[1].reshape(group_rows, DH)
    return (
        lax.all_to_all(attended, "head", split_axis=0, concat_axis=1, tiled=True),
        lax.all_to_all(query_grad, "head", split_axis=0, concat_axis=1, tiled=True),
        lax.all_to_all(key_grad, "head", split_axis=0, concat_axis=1, tiled=True),
        lax.all_to_all(value_grad, "head", split_axis=0, concat_axis=1, tiled=True),
    )


def solution(mesh):
    return jax.shard_map(
        per_device,
        mesh=mesh,
        in_specs=(
            P(("ctx", "head"), None),
            P(("ctx", "head"), None),
            P(("ctx", "head"), None),
            P(("ctx", "head"), None),
            P("head", "ctx", None),
        ),
        out_specs=(
            P(("ctx", "head"), None),
            P(("ctx", "head"), None),
            P(("ctx", "head"), None),
            P(("ctx", "head"), None),
        ),
        check_vma=False,
    )
```

profile of v0, /device:TPU:34, one launch (start us, length us, event | category | flops | bytes accessed | tf_op | source)
XLA Modules:
  0.0 783.4 jit_solution(1736343574578319628)
XLA Ops:
  2.6 8.7 %all-to-all-start.1 = ((bf16[144,16,128]{2,0,1:T(8,128)(2,1)}), bf16[144,16,128]{2,0,1:T(8,128)(2,1)S(1)}, u32[]{:S(2)}, u32[]{:S(2)}) async-start(bf16[144,16,128]{2,0,1:T(8,128)(2,1)} %copy_bitcast_fusion.6), calls=%async_computation.1 | async-start | bytes 1179648 | tf_op jit(solution)/shard_map/all_to_all | solution.py:60
  12.5 15.0 %all-to-all-done.1 = bf16[144,16,128]{2,0,1:T(8,128)(2,1)S(1)} async-done(((bf16[144,16,128]{2,0,1:T(8,128)(2,1)}), bf16[144,16,128]{2,0,1:T(8,128)(2,1)S(1)}, u32[]{:S(2)}, u32[]{:S(2)}) %all-to-all-start.1) | async-done | bytes 589856 | tf_op jit(solution)/shard_map/all_to_all | solution.py:60
  27.4 20.7 %all_to_all.134 = bf16[144,16,128]{2,0,1:T(8,128)(2,1)S(1)} all-to-all(bf16[144,16,128]{2,0,1:T(8,128)(2,1)S(1)} %copy_bitcast_fusion.5), channel_id=1, replica_groups=mesh['ctx'=16,'head'=16] {'head'}, dimensions={1} | all-to-all | bytes 1179648 | tf_op jit(solution)/shard_map/all_to_all | solution.py:61
  48.2 4.4 collective-permute-start
  53.5 5.8 all-to-all-start
  59.4 4.3 collective-permute-start.1
  64.3 2.0 copy_bitcast_fusion.4
  66.3 6.4 collective-permute-start.4
  72.6 2.4 collective-permute-start.3
  75.1 1.9 collective-permute-start.5
  77.0 17.3 %collective-permute-done = bf16[2304,2,128]{2,0,1:T(8,128)(2,1)} collective-permute-done((bf16[2304,2,128]{2,0,1:T(8,128)(2,1)S(1)}, bf16[2304,2,128]{2,0,1:T(8,128)(2,1)}, u32[]{:S(2)}, u32[]{:S(2)}) %collective-permute-start) | collective-permute-done | bytes 1179680 | tf_op jit(solution)/shard_map/ppermute | solution.py:20
  94.3 3.9 collective-permute-start.2
  98.2 2.4 bitcast_dynamic-update-slice_fusion.7
  100.6 32.0 %collective-permute-done.1 = bf16[2304,2,128]{2,0,1:T(8,128)(2,1)S(1)} collective-permute-done((bf16[2304,2,128]{2,0,1:T(8,128)(2,1)S(1)}, bf16[2304,2,128]{2,0,1:T(8,128)(2,1)S(1)}, u32[]{:S(2)}, u32[]{:S(2)}) %collective-permute-start.1) | collective-permute-done | bytes 1179680 | tf_op jit(solution)/shard_map/ppermute | solution.py:20
  133.6 134.5 %collective-permute-done.2 = bf16[2304,2,128]{2,0,1:T(8,128)(2,1)S(1)} collective-permute-done((bf16[2304,2,128]{2,0,1:T(8,128)(2,1)S(1)}, bf16[2304,2,128]{2,0,1:T(8,128)(2,1)S(1)}, u32[]{:S(2)}, u32[]{:S(2)}) %collective-permute-start.2) | collective-permute-done | bytes 1179680 | tf_op jit(solution)/shard_map/ppermute | solution.py:20
  271.5 6.3 all-to-all-start.3
  277.9 2.4 bitcast_dynamic-update-slice_fusion.2
  280.3 2.4 bitcast_dynamic-update-slice_fusion.1
  282.7 7.2 copy.83
  289.9 25.4 %copy.85 = bf16[84,192,2,128]{3,2,1,0:T(2,128)(2,1)} copy(bf16[84,192,2,128]{3,1,0,2:T(8,128)(2,1)} %bitcast.210) | data formatting | bytes 16515072 | tf_op jit(solution)/shard_map/while | solution.py:98
  315.3 7.7 broadcast_in_dim.32
  323.0 163.3 %while.14 = (s32[]{:T(128)}, f32[84,192,2,128]{3,1,2,0:T(8,128)}, bf16[3,4,192,128]{3,2,1,0:T(8,128)(2,1)}, bf16[3,4,192,128]{3,2,1,0:T(8,128)(2,1)S(1)}, s32[3]...) while((s32[]{:T(128)}, f32[84,192,2,128]{3,1,2,0:T(8,128)}, ...), condition=%wide.region_5.6_spmd, body=%wide.region_0.5_spmd.sunk | while | flops 2065120256 | bytes 104428088 | solution.py:98
  325.1 14.6 %gather_fusion = bf16[36,192,2,128]{3,2,1,0:T(2,128)(2,1)} fusion(bf16[84,192,2,128]{3,2,1,0:T(2,128)(2,1)} %get-tuple-element.235, s32[1024]{0:T(1024)S(1)} %pad_clamp_fusion.2), kind=kCustom, calls=%fused_computation.clone.1 | custom fusion | bytes 7078032 | tf_op jit(solution)/shard_map/while/body/eval_jaxpr/gather | solution.py:89
  339.7 2.9 copy.119
  343.8 1.7 fusion.69
  345.6 1.8 divide_convert_fusion.2
  347.4 1.4 multiply_reduce_fusion.2
  349.5 1.3 multiply_convert_fusion.2
  350.8 1.3 fusion.72
  354.3 3.8 pad_maximum_fusion.3
  358.0 19.2 %scatter_fusion = f32[84,192,2,128]{3,1,2,0:T(8,128)} fusion(f32[84,192,2,128]{3,1,2,0:T(8,128)} %get-tuple-element.214, s32[36]{0:T(128)S(1)} %fusion.67, f32[36,192,2,128]{3,1,2,0:T(8,128)} %pad_maximum_fusion.3), kind=kCustom, calls=%fused_computation.1.clone.1 | custom fusion | flops 1769472 | bytes 21233808 | tf_op jit(solution)/shard_map/while/body/eval_jaxpr/scatter-add | solution.py:94
  379.3 14.6 %gather_fusion = bf16[36,192,2,128]{3,2,1,0:T(2,128)(2,1)} fusion(bf16[84,192,2,128]{3,2,1,0:T(2,128)(2,1)} %get-tuple-element.235, s32[1024]{0:T(1024)S(1)} %pad_clamp_fusion.2), kind=kCustom, calls=%fused_computation.clone.1 | custom fusion | bytes 7078032 | tf_op jit(solution)/shard_map/while/body/eval_jaxpr/gather | solution.py:89
  393.9 2.9 copy.119
  398.0 1.7 fusion.69
  399.8 1.8 divide_convert_fusion.2
  401.6 1.4 multiply_reduce_fusion.2
  403.7 1.3 multiply_convert_fusion.2
  405.0 1.3 fusion.72
  408.4 3.8 pad_maximum_fusion.3
  412.2 19.2 %scatter_fusion = f32[84,192,2,128]{3,1,2,0:T(8,128)} fusion(f32[84,192,2,128]{3,1,2,0:T(8,128)} %get-tuple-element.214, s32[36]{0:T(128)S(1)} %fusion.67, f32[36,192,2,128]{3,1,2,0:T(8,128)} %pad_maximum_fusion.3), kind=kCustom, calls=%fused_computation.1.clone.1 | custom fusion | flops 1769472 | bytes 21233808 | tf_op jit(solution)/shard_map/while/body/eval_jaxpr/scatter-add | solution.py:94
  433.6 14.6 %gather_fusion = bf16[36,192,2,128]{3,2,1,0:T(2,128)(2,1)} fusion(bf16[84,192,2,128]{3,2,1,0:T(2,128)(2,1)} %get-tuple-element.235, s32[1024]{0:T(1024)S(1)} %pad_clamp_fusion.2), kind=kCustom, calls=%fused_computation.clone.1 | custom fusion | bytes 7078032 | tf_op jit(solution)/shard_map/while/body/eval_jaxpr/gather | solution.py:89
  448.2 2.9 copy.119
  452.3 1.7 fusion.69
  454.0 1.8 divide_convert_fusion.2
  455.9 1.4 multiply_reduce_fusion.2
  458.0 1.3 multiply_convert_fusion.2
  459.3 1.3 fusion.72
  462.7 3.8 pad_maximum_fusion.3
  466.5 19.8 %scatter_fusion = f32[84,192,2,128]{3,1,2,0:T(8,128)} fusion(f32[84,192,2,128]{3,1,2,0:T(8,128)} %get-tuple-element.214, s32[36]{0:T(128)S(1)} %fusion.67, f32[36,192,2,128]{3,1,2,0:T(8,128)} %pad_maximum_fusion.3), kind=kCustom, calls=%fused_computation.1.clone.1 | custom fusion | flops 1769472 | bytes 21233808 | tf_op jit(solution)/shard_map/while/body/eval_jaxpr/scatter-add | solution.py:94
  486.3 8.8 %fusion.32 = (bf16[12,192,2,128]{3,1,0,2:T(8,128)(2,1)S(1)}, bf16[12,192,2,128]{3,1,0,2:T(8,128)(2,1)S(1)}, bf16[12,192,2,128]{3,1,0,2:T(8,128)(2,1)}, bf16[12,1...) fusion(f32[84,192,2,128]{3,1,2,0:T(8,128)} %get-tuple-element.60), kind=kLoop, calls=%fused_computation.68 | loop fusion | bytes 16515072 | tf_op jit(solution)/shard_map/slice | solution.py:102
  495.1 2.8 collective-permute-start.11
  497.9 5.8 collective-permute-start.10
  503.7 1.9 collective-permute-start.9
  505.6 8.4 %collective-permute-start.8 = (bf16[2304,2,128]{2,0,1:T(8,128)(2,1)}, bf16[2304,2,128]{2,0,1:T(8,128)(2,1)}, u32[]{:S(2)}, u32[]{:S(2)}) collective-permute-start(bf16[2304,2,128]{2,0,1:T(8,128)(2,1)} %bitcast.45), channel_id=1, source_target_pairs={{16,0},{32,16},{48,32},{64,48},{80,64},{96,80},{112,96},{128,112},... | collective-permute-start | bytes 3538952 | tf_op jit(solution)/shard_map/ppermute | solution.py:20
  514.1 4.0 collective-permute-start.7
  518.1 13.1 %collective-permute-done.11 = bf16[2304,2,128]{2,0,1:T(8,128)(2,1)S(1)} collective-permute-done((bf16[2304,2,128]{2,0,1:T(8,128)(2,1)S(1)}, bf16[2304,2,128]{2,0,1:T(8,128)(2,1)S(1)}, u32[]{:S(2)}, u32[]{:S(2)}) %collective-permute-start.11) | collective-permute-done | bytes 1179680 | tf_op jit(solution)/shard_map/ppermute | solution.py:20
  531.2 1.9 collective-permute-start.6
  533.1 186.9 %all_to_all.135 = bf16[16,144,128]{2,1,0:T(8,128)(2,1)S(1)} all-to-all(bf16[16,144,128]{2,1,0:T(8,128)(2,1)S(1)} %bitcast.219), channel_id=1, replica_groups=mesh['ctx'=16,'head'=16] {'head'}, dimensions={0} | all-to-all | bytes 1179648 | tf_op jit(solution)/shard_map/all_to_all | solution.py:114
  720.1 4.7 all-to-all-start.4
  724.8 4.1 fusion.31
  729.9 11.4 %all-to-all-done.4 = bf16[16,144,128]{2,1,0:T(8,128)(2,1)S(1)} async-done(((bf16[16,144,128]{2,1,0:T(8,128)(2,1)}), bf16[16,144,128]{2,1,0:T(8,128)(2,1)S(1)}, u32[]{:S(2)}, u32[]{:S(2)}) %all-to-all-start.4) | async-done | bytes 589856 | tf_op jit(solution)/shard_map/all_to_all | solution.py:113
  741.3 20.8 %all_to_all.136 = bf16[16,144,128]{2,1,0:T(8,128)(2,1)S(1)} all-to-all(bf16[16,144,128]{2,1,0:T(8,128)(2,1)S(1)} %bitcast.217), channel_id=1, replica_groups=mesh['ctx'=16,'head'=16] {'head'}, dimensions={0} | all-to-all | bytes 1179648 | tf_op jit(solution)/shard_map/all_to_all | solution.py:115
  762.0 5.0 all-to-all-start.7
  769.7 12.9 %all-to-all-done.7 = bf16[16,144,128]{2,1,0:T(8,128)(2,1)S(1)} async-done(((bf16[16,144,128]{2,1,0:T(8,128)(2,1)}), bf16[16,144,128]{2,1,0:T(8,128)(2,1)S(1)}, u32[]{:S(2)}, u32[]{:S(2)}) %all-to-all-start.7) | async-done | bytes 589856 | tf_op jit(solution)/shard_map/all_to_all | solution.py:116
  (72 shorter events, 30.2 us)
Async XLA Ops:
  0.6 1.1 copy-start
  0.6 51.9 %copy-start.3 = (bf16[144,2048]{1,0:T(8,128)(2,1)S(1)}, bf16[144,2048]{1,0:T(8,128)(2,1)}, u32[]{:S(2)}) copy-start(bf16[144,2048]{1,0:T(8,128)(2,1)} %param.7) | copy-start | bytes 1769476
  2.6 24.8 %all-to-all-start.1 = ((bf16[144,16,128]{2,0,1:T(8,128)(2,1)}), bf16[144,16,128]{2,0,1:T(8,128)(2,1)S(1)}, u32[]{:S(2)}, u32[]{:S(2)}) async-start(bf16[144,16,128]{2,0,1:T(8,128)(2,1)} %copy_bitcast_fusion.6), calls=%async_computation.1 | async-start | bytes 1179648 | tf_op jit(solution)/shard_map/all_to_all | solution.py:60
  11.3 48.1 %copy-start.4 = (s32[1,12,9]{1,0,2:T(1,128)S(1)}, s32[1,12,9]{1,0,2:T(1,128)}, u32[]{:S(2)}) copy-start(s32[1,12,9]{1,0,2:T(1,128)} %param.11) | copy-start | bytes 1300
  48.2 46.1 %collective-permute-start = (bf16[2304,2,128]{2,0,1:T(8,128)(2,1)S(1)}, bf16[2304,2,128]{2,0,1:T(8,128)(2,1)}, u32[]{:S(2)}, u32[]{:S(2)}) collective-permute-start(bf16[2304,2,128]{2,0,1:T(8,128)(2,1)S(1)} %pad_maximum_fusion.1), channel_id=1, source_target_pairs={{0,48},{16,64},{32,80},{48,96},{64,112},{80,128},{96,144},{112,160... | collective-permute-start | bytes 3538952 | tf_op jit(solution)/shard_map/ppermute | solution.py:20
  53.5 218.0 %all-to-all-start = ((bf16[144,16,128]{2,0,1:T(8,128)(2,1)}), bf16[144,16,128]{2,0,1:T(8,128)(2,1)S(1)}, u32[]{:S(2)}, u32[]{:S(2)}) async-start(bf16[144,16,128]{2,0,1:T(8,128)(2,1)} %copy_bitcast_fusion.7), calls=%async_computation | async-start | bytes 1179648 | tf_op jit(solution)/shard_map/all_to_all | solution.py:59
  59.4 73.1 %collective-permute-start.1 = (bf16[2304,2,128]{2,0,1:T(8,128)(2,1)S(1)}, bf16[2304,2,128]{2,0,1:T(8,128)(2,1)S(1)}, u32[]{:S(2)}, u32[]{:S(2)}) collective-permute-start(bf16[2304,2,128]{2,0,1:T(8,128)(2,1)S(1)} %pad_maximum_fusion.1), channel_id=1, source_target_pairs={{0,32},{16,48},{32,64},{48,80},{64,96},{80,112},{96,128},{112,144}... | collective-permute-start | bytes 3538952 | tf_op jit(solution)/shard_map/ppermute | solution.py:20
  66.3 211.6 %collective-permute-start.4 = (bf16[2304,2,128]{2,0,1:T(8,128)(2,1)S(1)}, bf16[2304,2,128]{2,0,1:T(8,128)(2,1)}, u32[]{:S(2)}, u32[]{:S(2)}) collective-permute-start(bf16[2304,2,128]{2,0,1:T(8,128)(2,1)S(1)} %pad_maximum_fusion.1), channel_id=1, source_target_pairs={{32,0},{48,16},{64,32},{80,48},{96,64},{112,80},{128,96},{144,112}... | collective-permute-start | bytes 3538952 | tf_op jit(solution)/shard_map/ppermute | solution.py:20
  72.6 197.8 %collective-permute-start.3 = (bf16[2304,2,128]{2,0,1:T(8,128)(2,1)S(1)}, bf16[2304,2,128]{2,0,1:T(8,128)(2,1)S(1)}, u32[]{:S(2)}, u32[]{:S(2)}) collective-permute-start(bf16[2304,2,128]{2,0,1:T(8,128)(2,1)S(1)} %pad_maximum_fusion.1), channel_id=1, source_target_pairs={{16,0},{32,16},{48,32},{64,48},{80,64},{96,80},{112,96},{128,112},... | collective-permute-start | bytes 3538952 | tf_op jit(solution)/shard_map/ppermute | solution.py:20
  75.1 205.2 %collective-permute-start.5 = (bf16[2304,2,128]{2,0,1:T(8,128)(2,1)S(1)}, bf16[2304,2,128]{2,0,1:T(8,128)(2,1)}, u32[]{:S(2)}, u32[]{:S(2)}) collective-permute-start(bf16[2304,2,128]{2,0,1:T(8,128)(2,1)S(1)} %pad_maximum_fusion.1), channel_id=1, source_target_pairs={{48,0},{64,16},{80,32},{96,48},{112,64},{128,80},{144,96},{160,112... | collective-permute-start | bytes 3538952 | tf_op jit(solution)/shard_map/ppermute | solution.py:20
  94.3 173.9 %collective-permute-start.2 = (bf16[2304,2,128]{2,0,1:T(8,128)(2,1)S(1)}, bf16[2304,2,128]{2,0,1:T(8,128)(2,1)S(1)}, u32[]{:S(2)}, u32[]{:S(2)}) collective-permute-start(bf16[2304,2,128]{2,0,1:T(8,128)(2,1)S(1)} %pad_maximum_fusion.1), channel_id=1, source_target_pairs={{0,16},{16,32},{32,48},{48,64},{64,80},{80,96},{96,112},{112,128},... | collective-permute-start | bytes 3538952 | tf_op jit(solution)/shard_map/ppermute | solution.py:20
  271.5 43.7 %all-to-all-start.3 = ((bf16[144,16,128]{2,0,1:T(8,128)(2,1)}), bf16[144,16,128]{2,0,1:T(8,128)(2,1)S(1)}, u32[]{:S(2)}, u32[]{:S(2)}) async-start(bf16[144,16,128]{2,0,1:T(8,128)(2,1)} %copy_bitcast_fusion.4), calls=%async_computation.3 | async-start | bytes 1179648 | tf_op jit(solution)/shard_map/all_to_all | solution.py:62
  495.1 36.1 %collective-permute-start.11 = (bf16[2304,2,128]{2,0,1:T(8,128)(2,1)S(1)}, bf16[2304,2,128]{2,0,1:T(8,128)(2,1)S(1)}, u32[]{:S(2)}, u32[]{:S(2)}) collective-permute-start(bf16[2304,2,128]{2,0,1:T(8,128)(2,1)S(1)} %bitcast.218), channel_id=1, source_target_pairs={{0,48},{16,64},{32,80},{48,96},{64,112},{80,128},{96,144},{112,160... | collective-permute-start | bytes 3538952 | tf_op jit(solution)/shard_map/ppermute | solution.py:20
  497.9 226.9 %collective-permute-start.10 = (bf16[2304,2,128]{2,0,1:T(8,128)(2,1)}, bf16[2304,2,128]{2,0,1:T(8,128)(2,1)}, u32[]{:S(2)}, u32[]{:S(2)}) collective-permute-start(bf16[2304,2,128]{2,0,1:T(8,128)(2,1)} %bitcast.47), channel_id=1, source_target_pairs={{0,32},{16,48},{32,64},{48,80},{64,96},{80,112},{96,128},{112,144}... | collective-permute-start | bytes 3538952 | tf_op jit(solution)/shard_map/ppermute | solution.py:20
  503.7 221.1 %collective-permute-start.9 = (bf16[2304,2,128]{2,0,1:T(8,128)(2,1)}, bf16[2304,2,128]{2,0,1:T(8,128)(2,1)}, u32[]{:S(2)}, u32[]{:S(2)}) collective-permute-start(bf16[2304,2,128]{2,0,1:T(8,128)(2,1)} %bitcast.46), channel_id=1, source_target_pairs={{0,16},{16,32},{32,48},{48,64},{64,80},{80,96},{96,112},{112,128},... | collective-permute-start | bytes 3538952 | tf_op jit(solution)/shard_map/ppermute | solution.py:20
  505.6 219.2 %collective-permute-start.8 = (bf16[2304,2,128]{2,0,1:T(8,128)(2,1)}, bf16[2304,2,128]{2,0,1:T(8,128)(2,1)}, u32[]{:S(2)}, u32[]{:S(2)}) collective-permute-start(bf16[2304,2,128]{2,0,1:T(8,128)(2,1)} %bitcast.45), channel_id=1, source_target_pairs={{16,0},{32,16},{48,32},{64,48},{80,64},{96,80},{112,96},{128,112},... | collective-permute-start | bytes 3538952 | tf_op jit(solution)/shard_map/ppermute | solution.py:20
  514.1 210.7 %collective-permute-start.7 = (bf16[2304,2,128]{2,0,1:T(8,128)(2,1)}, bf16[2304,2,128]{2,0,1:T(8,128)(2,1)}, u32[]{:S(2)}, u32[]{:S(2)}) collective-permute-start(bf16[2304,2,128]{2,0,1:T(8,128)(2,1)} %bitcast.44), channel_id=1, source_target_pairs={{32,0},{48,16},{64,32},{80,48},{96,64},{112,80},{128,96},{144,112}... | collective-permute-start | bytes 3538952 | tf_op jit(solution)/shard_map/ppermute | solution.py:20
  531.2 1.9 copy-start.2
  531.2 193.6 %collective-permute-start.6 = (bf16[2304,2,128]{2,0,1:T(8,128)(2,1)}, bf16[2304,2,128]{2,0,1:T(8,128)(2,1)}, u32[]{:S(2)}, u32[]{:S(2)}) collective-permute-start(bf16[2304,2,128]{2,0,1:T(8,128)(2,1)} %bitcast.43), channel_id=1, source_target_pairs={{48,0},{64,16},{80,32},{96,48},{112,64},{128,80},{144,96},{160,112... | collective-permute-start | bytes 3538952 | tf_op jit(solution)/shard_map/ppermute | solution.py:20
  720.1 21.2 %all-to-all-start.4 = ((bf16[16,144,128]{2,1,0:T(8,128)(2,1)}), bf16[16,144,128]{2,1,0:T(8,128)(2,1)S(1)}, u32[]{:S(2)}, u32[]{:S(2)}) async-start(bf16[16,144,128]{2,1,0:T(8,128)(2,1)} %bitcast.38), calls=%async_computation.4 | async-start | bytes 1179648 | tf_op jit(solution)/shard_map/all_to_all | solution.py:113
  741.3 42.2 %copy-start.1 = (bf16[144,2048]{1,0:T(8,128)(2,1)S(1)}, bf16[144,2048]{1,0:T(8,128)(2,1)}, u32[]{:S(2)}) copy-start(bf16[144,2048]{1,0:T(8,128)(2,1)} %param.8) | copy-start | bytes 1769476
  762.0 20.5 %all-to-all-start.7 = ((bf16[16,144,128]{2,1,0:T(8,128)(2,1)}), bf16[16,144,128]{2,1,0:T(8,128)(2,1)S(1)}, u32[]{:S(2)}, u32[]{:S(2)}) async-start(bf16[16,144,128]{2,1,0:T(8,128)(2,1)} %bitcast.51), calls=%async_computation.7 | async-start | bytes 1179648 | tf_op jit(solution)/shard_map/all_to_all | solution.py:116
where the time goes:
time: 786 us; the launch traced here: 783 us
  waiting for transfers between devices  236 us (30%)
  blocking collectives  228 us (29%)
  local copies, waits for them, and re-layouts  129 us (16%)
  other arithmetic  86.1 us (11%)
  starting transfers between devices  78.6 us (10%)
  matrix products  22.1 us (3%)
    ppermute x12, waiting for transfers between devices, shifted(): return lax.ppermute(array, axis, pairs)  197 us
    all_to_all x1, blocking collectives, per_device(): lax.all_to_all(query_grad, 'head', split_axis=0, concat_axis=1, tiled=True)  187 us
    scatter-add x3, other arithmetic, advance(): grad_store = grad_store.at[chosen.reshape(-1)].add(both_parts)  58.2 us
    gather x6, local copies, waits for them, and re-layouts, advance(): gathered = tile_store[chosen]  52.5 us
    ppermute x12, starting transfers between devices, shifted(): return lax.ppermute(array, axis, pairs)  48.1 us
    while x1, local copies, waits for them, and re-layouts, per_device(): lax.scan(advance, zero_store, jnp.arange(GROUP_TILES // 4, dtype=jnp.int32))  25.4 us
    all_to_all x1, blocking collectives, per_device(): lax.all_to_all(key_grad, 'head', split_axis=0, concat_axis=1, tiled=True)  20.8 us
    all_to_all x1, blocking collectives, per_device(): lax.all_to_all(values, 'head', split_axis=1, concat_axis=0, tiled=True)  20.7 us
  transfers between devices with their start and end apart: 17, of which 7 were waited for; matrix products, arithmetic and copies ran while one was open for 7% of the time, Pallas kernels for 0%

commit v1 on v0

v1 whole, which is shorter than its diff:
```python
import math

import jax
import jax.numpy as jnp
from jax import lax
from jax.experimental import pallas as pl
from jax.experimental.pallas import tpu as pltpu
from jax.sharding import PartitionSpec as P

DH = 128
TILE = 192
HEADS = 16
PART = 48
ROWS = 144
COLS = 2 * TILE
SPAN = 4 * TILE
REACHED = 3 * TILE
NEG_FILL = -1e30
SCALE = 1.0 / math.sqrt(DH)
MESH = pl.DeviceIdType.MESH
VMEM_LIMIT = 60 * 1024 * 1024


def div(a, b):
    return lax.div(a, jnp.int32(b))


def rem(a, b):
    return lax.rem(a, jnp.int32(b))


def spot():
    ctx, sub = lax.axis_index("ctx"), lax.axis_index("head")
    core, z_hi, x = rem(ctx, 2), rem(div(ctx, 2), 2), div(ctx, 4)
    y, z_lo = rem(sub, 4), div(sub, 4)
    z = z_hi * 4 + z_lo
    head = 2 * z + div(y, 2)
    quarter = 2 * rem(y, 2) + core
    return dict(x=x, y=y, z=z, z_hi=z_hi, sub=sub, core=core, head=head, quarter=quarter)


def worker(x, head, quarter):
    z = div(head, 2)
    y = 2 * rem(head, 2) + div(quarter, 2)
    return (x * 4 + div(z, 4) * 2 + rem(quarter, 2), rem(z, 4) * 4 + y)


def copy_to(src, dst, send, recv, device):
    return pltpu.make_async_remote_copy(
        src_ref=src, dst_ref=dst, send_sem=send, recv_sem=recv, device_id=device, device_id_type=MESH
    )


def wait_bytes(ref, sem):
    pltpu.make_async_copy(ref, ref, sem).wait()


def gather_kernel(
    keys, values, queries, grads, flags, kv, qg, kinds, send_kv, recv_kv, send_qg, recv_qg, send_n, recv_n, kind_sems
):
    me = spot()
    x, z_hi, core, head, quarter = me["x"], me["z_hi"], me["core"], me["head"], me["quarter"]

    def part_place(k):
        at = me["sub"] * 3 + k
        tile = core * 12 + div(at, 4)
        column = rem(tile, 8)
        return div(tile, 8), div(column, 2), rem(column, 2), rem(at, 4)

    def send_head(target_head, own_head):
        for pair, out, send, recv, slab, shift in (
            ((keys, values), kv, send_kv, recv_kv, 1 + z_hi, 1),
            ((queries, grads), qg, send_qg, recv_qg, z_hi, 0),
        ):
            for k in range(3):
                row, to, side, part = part_place(k)
                first = pl.multiple_of((side + shift) * TILE + part * PART, 16)
                for a in range(2):
                    src = pair[a].at[pl.ds(k * PART, PART), pl.ds(pl.multiple_of(target_head * DH, DH), DH)]
                    dst = out.at[a, slab, row, pl.ds(first, PART), :]
                    if own_head:

                        @pl.when(to == quarter)
                        def _():
                            pltpu.make_async_copy(src, dst, recv).start()

                        @pl.when(to != quarter)
                        def _():
                            copy_to(src, dst, send, recv, worker(x, target_head, to)).start()

                    else:
                        copy_to(src, dst, send, recv, worker(x, target_head, to)).start()

    asker = (
        x * 4 + div(me["sub"], 8) * 2 + core,
        rem(div(me["sub"], 2), 4) * 4 + 2 * rem(me["sub"], 2) + z_hi,
    )
    own_kind = me["sub"] == head
    own_kind = jnp.logical_and(own_kind, rem(me["y"], 2) == z_hi)

    @pl.when(own_kind)
    def _():
        pltpu.make_async_copy(flags, kinds, kind_sems.at[1]).start()

    @pl.when(jnp.logical_not(own_kind))
    def _():
        copy_to(flags, kinds, kind_sems.at[0], kind_sems.at[1], asker).start()

    @pl.loop(1, HEADS)
    def _(step):
        send_head(rem(head + step, HEADS), False)

    send_head(head, True)

    own = kv.at[:, 1:3, :, TILE : TILE + COLS, :]
    wait_bytes(own, recv_kv)

    after = worker(rem(x + 1, 4), head, quarter)
    before = worker(rem(x + 3, 4), head, quarter)
    right = worker(x, head, rem(quarter + 1, 4))
    left = worker(x, head, rem(quarter + 3, 4))
    mine = slice(TILE, TILE + COLS)

    def halo(n, src, dst, device):
        return copy_to(src, dst, send_n.at[n], recv_n.at[n], device)

    forward = halo(0, kv.at[:, 2, :, mine, :], kv.at[:, 0, :, mine, :], after)
    backward = halo(1, kv.at[:, 1, :, mine, :], kv.at[:, 3, :, mine, :], before)
    forward.start()
    backward.start()
    hi, lo = slice(2 * TILE, 3 * TILE), slice(TILE, 2 * TILE)
    top, bottom = slice(3 * TILE, 4 * TILE), slice(0, TILE)
    inner = (
        halo(2, kv.at[:, 1:3, :, hi, :], kv.at[:, 1:3, :, bottom, :], right),
        halo(3, kv.at[:, 1:3, :, lo, :], kv.at[:, 1:3, :, top, :], left),
    )
    for c in inner:
        c.start()
    outer = []
    for n, slab, first in ((4, 0, forward), (6, 3, backward)):
        first.wait_recv()
        pair = (
            halo(n, kv.at[:, slab, :, hi, :], kv.at[:, slab, :, bottom, :], right),
            halo(n + 1, kv.at[:, slab, :, lo, :], kv.at[:, slab, :, top, :], left),
        )
        for c in pair:
            c.start()
        outer.extend(pair)
    for c in inner:
        c.wait()
    for c in outer:
        c.wait()
    forward.wait_send()
    backward.wait_send()
    wait_bytes(qg, recv_qg)
    own_parts = sum(
        (part_place(k)[1] == quarter).astype(jnp.int32) for k in range(3)
    )
    for count in range(4):

        @pl.when(own_parts == count)
        def _():
            sent = kv.at[:, 0, :, 0 : SPAN - 16 * count, :]
            wait_bytes(sent, send_kv)
            wait_bytes(sent, send_qg)

    wait_bytes(kinds, kind_sems.at[1])

    @pl.when(jnp.logical_not(own_kind))
    def _():
        wait_bytes(flags, kind_sems.at[0])


def work_kernel(kinds, kv, qg, outs, dkv, acc):
    me = spot()
    along_time = kinds[0, 0] > 0
    step_t = jnp.where(along_time, 1, 0)
    acc[...] = jnp.zeros_like(acc)

    def one_tile(t, masked, slab, row, side):
        first = pl.multiple_of(side * TILE, 64)
        q = qg[0, slab, row, pl.ds(first, TILE), :]
        g = qg[1, slab, row, pl.ds(first, TILE), :]
        span = pl.ds(first, REACHED)
        where = []
        scores = []
        for n in range(3):
            s_at = jnp.where(along_time, slab + n, slab + 1)
            r_at = jnp.where(along_time, row, jnp.clip(row + n - 1, 0, 2))
            where.append((s_at, r_at))
            k_rows = kv[0, s_at, r_at, span, :]
            s = lax.dot_general(q, k_rows, (((1,), (1,)), ((), ())), preferred_element_type=jnp.float32)
            if masked:
                ok_time = jnp.logical_and(2 * me["x"] + slab + n - 1 >= 0, 2 * me["x"] + slab + n - 1 < 8)
                ok_row = jnp.logical_and(row + n - 1 >= 0, row + n - 1 < 3)
                ok = jnp.where(along_time, ok_time.astype(jnp.int32), ok_row.astype(jnp.int32))
                column = 2 * me["quarter"] + side
                low = jnp.where(column > 0, 0, TILE)
                high = jnp.where(column < 7, REACHED, 2 * TILE) * ok
                lane = lax.broadcasted_iota(jnp.int32, s.shape, 1)
                s = jnp.where(jnp.logical_and(lane >= low, lane < high), s, NEG_FILL)
            scores.append(s)
        top = jnp.max(jnp.maximum(jnp.maximum(scores[0], scores[1]), scores[2]), axis=1, keepdims=True)
        raised = [jnp.exp((s - top) * SCALE) for s in scores]
        total = jnp.sum(raised[0] + raised[1] + raised[2], axis=1, keepdims=True)
        share = 1.0 / total
        weights = [(r * share).astype(jnp.bfloat16) for r in raised]
        attended = jnp.zeros((TILE, DH), jnp.float32)
        for n in range(3):
            v_rows = kv[1, where[n][0], where[n][1], span, :]
            attended += jnp.dot(weights[n], v_rows, preferred_element_type=jnp.float32)
        attended = attended.astype(jnp.bfloat16)
        outs[0, slab, row, pl.ds(first, TILE), :] = attended
        delta = jnp.sum(g.astype(jnp.float32) * attended.astype(jnp.float32), axis=1, keepdims=True)
        q_grad = jnp.zeros((TILE, DH), jnp.float32)
        for n in range(3):
            s_at, r_at = where[n]
            v_rows = kv[1, s_at, r_at, span, :]
            w_grad = lax.dot_general(g, v_rows, (((1,), (1,)), ((), ())), preferred_element_type=jnp.float32)
            s_grad = (weights[n].astype(jnp.float32) * (w_grad - delta) * SCALE).astype(jnp.bfloat16)
            k_rows = kv[0, s_at, r_at, span, :]
            q_grad += jnp.dot(s_grad, k_rows, preferred_element_type=jnp.float32)
            acc[0, s_at, r_at, span, :] += lax.dot_general(
                s_grad, q, (((0,), (0,)), ((), ())), preferred_element_type=jnp.float32
            )
            acc[1, s_at, r_at, span, :] += lax.dot_general(
                weights[n], g, (((0,), (0,)), ((), ())), preferred_element_type=jnp.float32
            )
        outs[1, slab, row, pl.ds(first, TILE), :] = q_grad.astype(jnp.bfloat16)

    @pl.loop(0, 12)
    def _(t):
        slab, row, side = div(t, 6), rem(div(t, 2), 3), rem(t, 2)
        column = 2 * me["quarter"] + side
        slab_at = 2 * me["x"] + slab
        inside = jnp.where(
            along_time,
            jnp.logical_and(slab_at > 0, slab_at < 7).astype(jnp.int32),
            (row == 1).astype(jnp.int32),
        )
        full = jnp.logical_and(inside == 1, jnp.logical_and(column > 0, column < 7))

        @pl.when(full)
        def _():
            one_tile(t, False, slab, row, side)

        @pl.when(jnp.logical_not(full))
        def _():
            one_tile(t, True, slab, row, side)

    for s_at in range(4):
        for r_at in range(3):
            for a in range(2):
                dkv[a, s_at, r_at] = acc[a, s_at, r_at].astype(jnp.bfloat16)


def scatter_kernel(
    outs, dkv, attended, q_grad, k_grad, v_grad, from_side, from_slab, summed, final,
    send_o, recv_o, send_d, recv_d, send_n, recv_n
):
    me = spot()
    x, head, quarter = me["x"], me["head"], me["quarter"]

    def send_parts(src_of, targets, send, recv):
        @pl.loop(0, 48)
        def _(step):
            n = rem(step + 3 * head, 48)
            slab, row, side, part = div(n, 24), div(rem(n, 24), 8), rem(div(n, 4), 2), rem(n, 4)
            tile = row * 8 + 2 * quarter + side
            at = rem(tile, 12) * 4 + part
            core, sub, k = div(tile, 12), div(at, 3), rem(at, 3)
            ctx = x * 4 + slab * 2 + core
            self_part = jnp.logical_and(ctx == lax.axis_index("ctx"), sub == me["sub"])
            first = pl.multiple_of(side * TILE + part * PART, 16)
            for a in range(2):
                src = src_of(a, slab, row, pl.ds(first, PART))
                dst = targets[a].at[
                    pl.ds(pl.multiple_of(k * PART, 16), PART), pl.ds(pl.multiple_of(head * DH, DH), DH)
                ]

                @pl.when(self_part)
                def _():
                    pltpu.make_async_copy(src, dst, recv).start()

                @pl.when(jnp.logical_not(self_part))
                def _():
                    copy_to(src, dst, send, recv, (ctx, sub)).start()

    send_parts(lambda a, s, r, rows: outs.at[a, s, r, rows, :], (attended, q_grad), send_o, recv_o.at[0])

    right = worker(x, head, rem(quarter + 1, 4))
    left = worker(x, head, rem(quarter + 3, 4))
    to_left = copy_to(dkv.at[:, :, :, 0:TILE, :], from_side.at[1], send_n.at[1], recv_n.at[1], left)
    to_right = copy_to(
        dkv.at[:, :, :, 3 * TILE : 4 * TILE, :], from_side.at[0], send_n.at[0], recv_n.at[0], right
    )
    @pl.when(quarter > 0)
    def _():
        to_left.start()

    @pl.when(quarter < 3)
    def _():
        to_right.start()

    for side in range(2):
        has = quarter > 0 if side == 0 else quarter < 3
        here = slice((1 + side) * TILE, (2 + side) * TILE)
        there = slice(side * TILE, (1 + side) * TILE)

        @pl.when(has)
        def _():
            wait_bytes(from_side.at[side], recv_n.at[side])
            for a in range(2):
                for s in range(4):
                    summed[a, s, :, there, :] = (
                        dkv[a, s, :, here, :].astype(jnp.float32) + from_side[side, a, s].astype(jnp.float32)
                    ).astype(jnp.bfloat16)

        @pl.when(jnp.logical_not(has))
        def _():
            for a in range(2):
                for s in range(4):
                    summed[a, s, :, there, :] = dkv[a, s, :, here, :]

    after = worker(rem(x + 1, 4), head, quarter)
    before = worker(rem(x + 3, 4), head, quarter)
    to_after = copy_to(summed.at[:, 3], from_slab.at[0], send_n.at[2], recv_n.at[2], after)
    to_before = copy_to(summed.at[:, 0], from_slab.at[1], send_n.at[3], recv_n.at[3], before)

    @pl.when(x < 3)
    def _():
        to_after.start()

    @pl.when(x > 0)
    def _():
        to_before.start()

    for slab in range(2):
        has = x > 0 if slab == 0 else x < 3

        @pl.when(has)
        def _():
            wait_bytes(from_slab.at[slab], recv_n.at[2 + slab])
            for a in range(2):
                final[a, slab] = (
                    summed[a, 1 + slab].astype(jnp.float32) + from_slab[slab, a].astype(jnp.float32)
                ).astype(jnp.bfloat16)

        @pl.when(jnp.logical_not(has))
        def _():
            for a in range(2):
                final[a, slab] = summed[a, 1 + slab]

    send_parts(lambda a, s, r, rows: final.at[a, s, r, rows, :], (k_grad, v_grad), send_d, recv_d.at[0])

    @pl.when(quarter > 0)
    def _():
        to_left.wait_send()

    @pl.when(quarter < 3)
    def _():
        to_right.wait_send()

    @pl.when(x < 3)
    def _():
        to_after.wait_send()

    @pl.when(x > 0)
    def _():
        to_before.wait_send()

    def own_part(k):
        at = me["sub"] * 3 + k
        tile = me["core"] * 12 + div(at, 4)
        return (div(rem(tile, 8), 2) == quarter).astype(jnp.int32)

    own_parts = own_part(0) + own_part(1) + own_part(2)
    for count in range(4):

        @pl.when(own_parts == count)
        def _():
            sent = dkv.at[:, 0, :, 0 : SPAN - 16 * count, :]
            wait_bytes(sent, send_o)
            wait_bytes(sent, send_d)

    wait_bytes(outs, recv_o.at[0])
    wait_bytes(final, recv_d.at[0])


def per_device(queries, keys, values, out_grad, key_tiles):
    ctx = lax.axis_index("ctx")
    own_slab = ctx // 2
    lists = key_tiles[0]
    along_time = jnp.any(jnp.logical_and(lists >= 0, lists // 24 != own_slab))
    flags = jnp.broadcast_to(along_time.astype(jnp.int32), (8, 128))

    anywhere = pl.BlockSpec(memory_space=pl.ANY)
    vmem = pl.BlockSpec(memory_space=pltpu.VMEM)
    kv, qg, kinds = pl.pallas_call(
        gather_kernel,
        name="gather_heads",
        out_shape=(
            jax.ShapeDtypeStruct((2, 4, 3, SPAN, DH), jnp.bfloat16),
            jax.ShapeDtypeStruct((2, 2, 3, COLS, DH), jnp.bfloat16),
            jax.ShapeDtypeStruct((8, 128), jnp.int32),
        ),
        in_specs=[anywhere] * 5,
        out_specs=(anywhere, anywhere, anywhere),
        scratch_shapes=[
            pltpu.SemaphoreType.DMA,
            pltpu.SemaphoreType.DMA,
            pltpu.SemaphoreType.DMA,
            pltpu.SemaphoreType.DMA,
            pltpu.SemaphoreType.DMA((8,)),
            pltpu.SemaphoreType.DMA((8,)),
            pltpu.SemaphoreType.DMA((2,)),
        ],
        compiler_params=pltpu.CompilerParams(has_side_effects=True),
    )(keys, values, queries, out_grad, flags)

    outs, dkv = pl.pallas_call(
        work_kernel,
        name="tile_attention",
        out_shape=(
            jax.ShapeDtypeStruct((2, 2, 3, COLS, DH), jnp.bfloat16),
            jax.ShapeDtypeStruct((2, 4, 3, SPAN, DH), jnp.bfloat16),
        ),
        in_specs=[pl.BlockSpec(memory_space=pltpu.SMEM), vmem, vmem],
        out_specs=(vmem, vmem),
        scratch_shapes=[pltpu.VMEM((2, 4, 3, SPAN, DH), jnp.float32)],
        compiler_params=pltpu.CompilerParams(vmem_limit_bytes=VMEM_LIMIT),
    )(kinds, kv, qg)

    token_block = jax.ShapeDtypeStruct((ROWS, HEADS * DH), jnp.bfloat16)
    return pl.pallas_call(
        scatter_kernel,
        name="scatter_heads",
        out_shape=(token_block,) * 4,
        in_specs=[anywhere, vmem],
        out_specs=(anywhere,) * 4,
        scratch_shapes=[
            pltpu.VMEM((2, 2, 4, 3, TILE, DH), jnp.bfloat16),
            pltpu.VMEM((2, 2, 3, COLS, DH), jnp.bfloat16),
            pltpu.VMEM((2, 4, 3, COLS, DH), jnp.bfloat16),
            pltpu.VMEM((2, 2, 3, COLS, DH), jnp.bfloat16),
            pltpu.SemaphoreType.DMA,
            pltpu.SemaphoreType.DMA((1,)),
            pltpu.SemaphoreType.DMA,
            pltpu.SemaphoreType.DMA((1,)),
            pltpu.SemaphoreType.DMA((4,)),
            pltpu.SemaphoreType.DMA((4,)),
        ],
        compiler_params=pltpu.CompilerParams(has_side_effects=True, vmem_limit_bytes=VMEM_LIMIT),
    )(outs, dkv)


def solution(mesh):
    token_spec = P(("ctx", "head"), None)
    return jax.shard_map(
        per_device,
        mesh=mesh,
        in_specs=(token_spec,) * 4 + (P("head", "ctx", None),),
        out_specs=(token_spec,) * 4,
        check_vma=False,
    )
```

time: 786 us -> 221 us (0.28)
  the two profiles are of different devices: /device:TPU:34 before, /device:TPU:1 now
where the time goes in v1:
time: 221 us
  Pallas kernels  210 us (95%)
  local copies, waits for them, and re-layouts  9.08 us (4%)
    pallas_call x1, Pallas kernels, per_device(): pl.pallas_call(gather_kernel, name='gather_heads', out_shape=(jax.ShapeDt...  94.6 us
    pallas_call x1, Pallas kernels, per_device(): pl.pallas_call(scatter_kernel, name='scatter_heads', out_shape=(token_blo...  80.4 us
    pallas_call x1, Pallas kernels, per_device(): pl.pallas_call(work_kernel, name='tile_attention', out_shape=(jax.ShapeDt...  35 us
    unnamed x5, local copies, waits for them, and re-layouts  8.49 us

profile of v1, /device:TPU:1, one launch (start us, length us, event | category | flops | bytes accessed | tf_op | source)
XLA Modules:
  0.0 221.0 jit_solution(15848614711562397902)
XLA Ops:
  0.6 0.8 copy.9
  1.4 0.6 fusion.3
  2.7 0.6 broadcast_in_dim.3.flags
  3.3 94.6 %gather_heads.1 = (bf16[2,4,3,768,128]{4,3,2,1,0:T(8,128)(2,1)}, bf16[2,2,3,384,128]{4,3,2,1,0:T(8,128)(2,1)}, s32[8,128]{1,0:T(8,128)}) custom-call(bf16[144,2048]{1,0:T(8,128)(2,1)} %keys.1, bf16[144,2048]{1,0:T(8,128)(2,1)} %values.1, bf16[144,2048]{1,0:T(8,128)(2,1)} %queries.1, bf16[144,2048]{1,0:T(8,128)(2,1)} %grads.1, s32[8,128]{1,0:T(8,128)} %broadcast_in_dim.3.flags), custom_call_target="tpu_custom_call" | custom-call | tf_op jit(solution)/shard_map/gather_heads/pallas_call | solution.py:399
  97.9 35.0 %tile_attention.1 = (bf16[2,2,3,384,128]{4,3,2,1,0:T(8,128)(2,1)}, bf16[2,4,3,768,128]{4,3,2,1,0:T(8,128)(2,1)}) custom-call(s32[8,128]{1,0:T(8,128)} %get-tuple-element.9.kinds, bf16[2,4,3,768,128]{4,3,2,1,0:T(8,128)(2,1)} %get-tuple-element.10.kv, bf16[2,2,3,384,128]{4,3,2,1,0:T(8,128)(2,1)} %get-tuple-element.11.qg), custom_call_target="tpu_custom_call" | custom-call | tf_op jit(solution)/shard_map/tile_attention/pallas_call | solution.py:421
  132.9 80.4 %scatter_heads.1 = (bf16[144,2048]{1,0:T(8,128)(2,1)}, bf16[144,2048]{1,0:T(8,128)(2,1)}, bf16[144,2048]{1,0:T(8,128)(2,1)}, bf16[144,2048]{1,0:T(8,128)(2,1)}) custom-call(bf16[2,2,3,384,128]{4,3,2,1,0:T(8,128)(2,1)} %get-tuple-element.12.outs, bf16[2,4,3,768,128]{4,3,2,1,0:T(8,128)(2,1)} %get-tuple-element.13.dkv), custom_call_target="tpu_custom_call" | custom-call | tf_op jit(solution)/shard_map/scatter_heads/pallas_call | solution.py:435
  213.3 1.9 copy.17
  215.2 1.9 copy.18
  217.2 1.9 copy.19
  219.1 1.9 copy.20

commit v2 on v1

--- a/solution.py
+++ b/solution.py
@@ -51,6 +51,24 @@
     )
 
 
+def greet(me):
+    barrier = pltpu.get_barrier_semaphore()
+    x = me["x"]
+    own = me["sub"] * 4 + me["z_hi"] * 2 + me["core"]
+
+    @pl.loop(1, 64)
+    def _(step):
+        other = rem(own + step, 64)
+        device = (x * 4 + rem(other, 4), div(other, 4))
+        pl.semaphore_signal(barrier, inc=1, device_id=device, device_id_type=MESH)
+
+    here = me["z_hi"] * 2 + me["core"]
+    for step in (1, 3):
+        device = (rem(x + step, 4) * 4 + here, me["sub"])
+        pl.semaphore_signal(barrier, inc=1, device_id=device, device_id_type=MESH)
+    pl.semaphore_wait(barrier, 65)
+
+
 def wait_bytes(ref, sem):
     pltpu.make_async_copy(ref, ref, sem).wait()
 
@@ -67,11 +85,10 @@
         column = rem(tile, 8)
         return div(tile, 8), div(column, 2), rem(column, 2), rem(at, 4)
 
-    def send_head(target_head, own_head):
-        for pair, out, send, recv, slab, shift in (
-            ((keys, values), kv, send_kv, recv_kv, 1 + z_hi, 1),
-            ((queries, grads), qg, send_qg, recv_qg, z_hi, 0),
-        ):
+    greet(me)
+
+    def send_head(which, target_head, own_head):
+        for pair, out, send, recv, slab, shift in (which,):
             for k in range(3):
                 row, to, side, part = part_place(k)
                 first = pl.multiple_of((side + shift) * TILE + part * PART, 16)
@@ -106,50 +123,66 @@
     def _():
         copy_to(flags, kinds, kind_sems.at[0], kind_sems.at[1], asker).start()
 
-    @pl.loop(1, HEADS)
-    def _(step):
-        send_head(rem(head + step, HEADS), False)
-
-    send_head(head, True)
+    for which in (
+        ((keys, values), kv, send_kv, recv_kv, 1 + z_hi, 1),
+        ((queries, grads), qg, send_qg, recv_qg, z_hi, 0),
+    ):
+        pl.loop(1, HEADS)(lambda step: send_head(which, rem(head + step, HEADS), False))
+        send_head(which, head, True)
 
     own = kv.at[:, 1:3, :, TILE : TILE + COLS, :]
     wait_bytes(own, recv_kv)
 
     after = worker(rem(x + 1, 4), head, quarter)
     before = worker(rem(x + 3, 4), head, quarter)
-    right = worker(x, head, rem(quarter + 1, 4))
-    left = worker(x, head, rem(quarter + 3, 4))
     mine = slice(TILE, TILE + COLS)
+    hi, lo = slice(2 * TILE, 3 * TILE), slice(TILE, 2 * TILE)
+    top, bottom = slice(3 * TILE, 4 * TILE), slice(0, TILE)
 
     def halo(n, src, dst, device):
         return copy_to(src, dst, send_n.at[n], recv_n.at[n], device)
+
+    def side_halos(n, slabs, action):
+        to_right, to_left = kv.at[:, slabs, :, hi, :], kv.at[:, slabs, :, lo, :]
+        at_right, at_left = kv.at[:, slabs, :, bottom, :], kv.at[:, slabs, :, top, :]
+
+        def send(k, src, dst, to):
+            copy = copy_to(src, dst, send_n.at[n + k], recv_n.at[n + k % 2], worker(x, head, to))
+            getattr(copy, action)()
+
+        @pl.when(quarter < 3)
+        def _():
+            send(0, to_right, at_right, rem(quarter + 1, 4))
+
+        @pl.when(quarter > 0)
+        def _():
+            send(1, to_left, at_left, rem(quarter + 3, 4))
+
+        @pl.when(quarter == 1)
+        def _():
+            send(2, to_right, at_right, quarter - 1)
+
+        @pl.when(quarter == 2)
+        def _():
+            send(3, to_left, at_left, quarter + 1)
+
+        if action == "wait_send":
+            wait_bytes(at_right, recv_n.at[n])
+            wait_bytes(at_left, recv_n.at[n + 1])
 
     forward = halo(0, kv.at[:, 2, :, mine, :], kv.at[:, 0, :, mine, :], after)
     backward = halo(1, kv.at[:, 1, :, mine, :], kv.at[:, 3, :, mine, :], before)
     forward.start()
     backward.start()
-    hi, lo = slice(2 * TILE, 3 * TILE), slice(TILE, 2 * TILE)
-    top, bottom = slice(3 * TILE, 4 * TILE), slice(0, TILE)
-    inner = (
-        halo(2, kv.at[:, 1:3, :, hi, :], kv.at[:, 1:3, :, bottom, :], right),
-        halo(3, kv.at[:, 1:3, :, lo, :], kv.at[:, 1:3, :, top, :], left),
-    )
-    for c in inner:
-        c.start()
-    outer = []
-    for n, slab, first in ((4, 0, forward), (6, 3, backward)):
-        first.wait_recv()
-        pair = (
-            halo(n, kv.at[:, slab, :, hi, :], kv.at[:, slab, :, bottom, :], right),
-            halo(n + 1, kv.at[:, slab, :, lo, :], kv.at[:, slab, :, top, :], left),
-        )
-        for c in pair:
-            c.start()
-        outer.extend(pair)
-    for c in inner:
-        c.wait()
-    for c in outer:
-        c.wait()
+    inner = slice(1, 3)
+    side_halos(2, inner, "start")
+    forward.wait_recv()
+    side_halos(6, 0, "start")
+    backward.wait_recv()
+    side_halos(10, 3, "start")
+    side_halos(2, inner, "wait_send")
+    side_halos(6, 0, "wait_send")
+    side_halos(10, 3, "wait_send")
     forward.wait_send()
     backward.wait_send()
     wait_bytes(qg, recv_qg)
@@ -260,6 +293,7 @@
 ):
     me = spot()
     x, head, quarter = me["x"], me["head"], me["quarter"]
+    greet(me)
 
     def send_parts(src_of, targets, send, recv):
         @pl.loop(0, 48)
@@ -385,6 +419,19 @@
 
     wait_bytes(outs, recv_o.at[0])
     wait_bytes(final, recv_d.at[0])
+
+
+def place_kernel(*refs):
+    sources, results, buffers, sems = refs[:4], refs[4:8], refs[8:12], refs[12]
+    loads = [pltpu.make_async_copy(s, b, sems.at[n]) for n, (s, b) in enumerate(zip(sources, buffers))]
+    stores = [pltpu.make_async_copy(b, r, sems.at[4 + n]) for n, (b, r) in enumerate(zip(buffers, results))]
+    for c in loads:
+        c.start()
+    for load, store in zip(loads, stores):
+        load.wait()
+        store.start()
+    for c in stores:
+        c.wait()
 
 
 def per_device(queries, keys, values, out_grad, key_tiles):
@@ -411,11 +458,11 @@
             pltpu.SemaphoreType.DMA,
             pltpu.SemaphoreType.DMA,
             pltpu.SemaphoreType.DMA,
-            pltpu.SemaphoreType.DMA((8,)),
-            pltpu.SemaphoreType.DMA((8,)),
+            pltpu.SemaphoreType.DMA((14,)),
+            pltpu.SemaphoreType.DMA((14,)),
             pltpu.SemaphoreType.DMA((2,)),
         ],
-        compiler_params=pltpu.CompilerParams(has_side_effects=True),
+        compiler_params=pltpu.CompilerParams(has_side_effects=True, collective_id=0),
     )(keys, values, queries, out_grad, flags)
 
     outs, dkv = pl.pallas_call(
@@ -432,7 +479,7 @@
     )(kinds, kv, qg)
 
     token_block = jax.ShapeDtypeStruct((ROWS, HEADS * DH), jnp.bfloat16)
-    return pl.pallas_call(
+    blocks = pl.pallas_call(
         scatter_kernel,
         name="scatter_heads",
         out_shape=(token_block,) * 4,
@@ -450,8 +497,17 @@
             pltpu.SemaphoreType.DMA((4,)),
             pltpu.SemaphoreType.DMA((4,)),
         ],
-        compiler_params=pltpu.CompilerParams(has_side_effects=True, vmem_limit_bytes=VMEM_LIMIT),
+        compiler_params=pltpu.CompilerParams(has_side_effects=True, collective_id=1, vmem_limit_bytes=VMEM_LIMIT),
     )(outs, dkv)
+    return pl.pallas_call(
+        place_kernel,
+        name="place_results",
+        out_shape=(token_block,) * 4,
+        in_specs=[anywhere] * 4,
+        out_specs=(anywhere,) * 4,
+        scratch_shapes=[pltpu.VMEM((ROWS, HEADS * DH), jnp.bfloat16)] * 4 + [pltpu.SemaphoreType.DMA((8,))],
+        compiler_params=pltpu.CompilerParams(vmem_limit_bytes=VMEM_LIMIT),
+    )(*blocks)
 
 
 def solution(mesh):

time: 221 us -> 178 us (0.81)
  the two profiles are of different devices: /device:TPU:1 before, /device:TPU:11 now
where the time goes in v2:
time: 178 us
  Pallas kernels  175 us (98%)
    pallas_call x1, Pallas kernels, per_device(): pl.pallas_call(scatter_kernel, name='scatter_heads', out_shape=(token_blo...  74.5 us
    pallas_call x1, Pallas kernels, per_device(): pl.pallas_call(gather_kernel, name='gather_heads', out_shape=(jax.ShapeDt...  62.6 us
    pallas_call x1, Pallas kernels, per_device(): pl.pallas_call(work_kernel, name='tile_attention', out_shape=(jax.ShapeDt...  35.2 us

profile of v2, /device:TPU:11, one launch (start us, length us, event | category | flops | bytes accessed | tf_op | source)
XLA Modules:
  0.0 178.2 jit_solution(16816783765692361993)
XLA Ops:
  0.6 0.8 copy.9
  1.4 0.6 fusion.3
  2.7 0.6 broadcast_in_dim.3.flags
  3.3 62.6 %gather_heads.1 = (bf16[2,4,3,768,128]{4,3,2,1,0:T(8,128)(2,1)}, bf16[2,2,3,384,128]{4,3,2,1,0:T(8,128)(2,1)}, s32[8,128]{1,0:T(8,128)}) custom-call(bf16[144,2048]{1,0:T(8,128)(2,1)} %keys.1, bf16[144,2048]{1,0:T(8,128)(2,1)} %values.1, bf16[144,2048]{1,0:T(8,128)(2,1)} %queries.1, bf16[144,2048]{1,0:T(8,128)(2,1)} %grads.1, s32[8,128]{1,0:T(8,128)} %broadcast_in_dim.3.flags), custom_call_target="tpu_custom_call" | custom-call | tf_op jit(solution)/shard_map/gather_heads/pallas_call | solution.py:446
  65.9 35.2 %tile_attention.1 = (bf16[2,2,3,384,128]{4,3,2,1,0:T(8,128)(2,1)}, bf16[2,4,3,768,128]{4,3,2,1,0:T(8,128)(2,1)}) custom-call(s32[8,128]{1,0:T(8,128)} %get-tuple-element.13.kinds, bf16[2,4,3,768,128]{4,3,2,1,0:T(8,128)(2,1)} %get-tuple-element.14.kv, bf16[2,2,3,384,128]{4,3,2,1,0:T(8,128)(2,1)} %get-tuple-element.15.qg), custom_call_target="tpu_custom_call" | custom-call | tf_op jit(solution)/shard_map/tile_attention/pallas_call | solution.py:468
  101.1 74.5 %scatter_heads.1 = (bf16[144,2048]{1,0:T(8,128)(2,1)}, bf16[144,2048]{1,0:T(8,128)(2,1)}, bf16[144,2048]{1,0:T(8,128)(2,1)}, bf16[144,2048]{1,0:T(8,128)(2,1)}) custom-call(bf16[2,2,3,384,128]{4,3,2,1,0:T(8,128)(2,1)} %get-tuple-element.16.outs, bf16[2,4,3,768,128]{4,3,2,1,0:T(8,128)(2,1)} %get-tuple-element.17.dkv), custom_call_target="tpu_custom_call" | custom-call | tf_op jit(solution)/shard_map/scatter_heads/pallas_call | solution.py:482
  175.6 2.5 %place_results.1 = (bf16[144,2048]{1,0:T(8,128)(2,1)}, bf16[144,2048]{1,0:T(8,128)(2,1)}, bf16[144,2048]{1,0:T(8,128)(2,1)}, bf16[144,2048]{1,0:T(8,128)(2,1)}) custom-call(bf16[144,2048]{1,0:T(8,128)(2,1)} %get-tuple-element.18.refs_0_, bf16[144,2048]{1,0:T(8,128)(2,1)} %get-tuple-element.19.refs_1_, bf16[144,2048]{1,0:T(8,128)(2,1)} %get-tuple-element.20.refs_2_, ...), custom_call_target="tpu_custom_call" | custom-call | tf_op jit(solution)/shard_map/place_results/pallas_call | solution.py:502

commit v3 on v0

v3 whole, which is shorter than its diff:
```python
import math

import jax
import jax.numpy as jnp
from jax import lax
from jax.experimental import pallas as pl
from jax.experimental.pallas import tpu as pltpu
from jax.sharding import PartitionSpec as P

DH = 128
TILE = 192
HEADS = 16
PART = 48
ROWS = 144
COLS = 2 * TILE
SPAN = 4 * TILE
REACHED = 3 * TILE
NEG_FILL = -1e30
SCALE = 1.0 / math.sqrt(DH)
LOG2E = 1.0 / math.log(2.0)
MESH = pl.DeviceIdType.MESH
VMEM_LIMIT = 60 * 1024 * 1024


def div(a, b):
    return lax.div(a, jnp.int32(b))


def rem(a, b):
    return lax.rem(a, jnp.int32(b))


def spot():
    ctx, sub = lax.axis_index("ctx"), lax.axis_index("head")
    core, z_hi, x = rem(ctx, 2), rem(div(ctx, 2), 2), div(ctx, 4)
    y, z_lo = rem(sub, 4), div(sub, 4)
    z = z_hi * 4 + z_lo
    head = 2 * z + div(y, 2)
    quarter = 2 * rem(y, 2) + core
    return dict(x=x, y=y, z=z, z_hi=z_hi, sub=sub, core=core, head=head, quarter=quarter)


def worker(x, head, quarter):
    z = div(head, 2)
    y = 2 * rem(head, 2) + div(quarter, 2)
    return (x * 4 + div(z, 4) * 2 + rem(quarter, 2), rem(z, 4) * 4 + y)


def copy_to(src, dst, send, recv, device):
    return pltpu.make_async_remote_copy(
        src_ref=src, dst_ref=dst, send_sem=send, recv_sem=recv, device_id=device, device_id_type=MESH
    )


def greet(me):
    barrier = pltpu.get_barrier_semaphore()
    x = me["x"]
    own = me["sub"] * 4 + me["z_hi"] * 2 + me["core"]

    @pl.loop(1, 64)
    def _(step):
        other = rem(own + step, 64)
        device = (x * 4 + rem(other, 4), div(other, 4))
        pl.semaphore_signal(barrier, inc=1, device_id=device, device_id_type=MESH)

    here = me["z_hi"] * 2 + me["core"]
    for step in (1, 3):
        device = (rem(x + step, 4) * 4 + here, me["sub"])
        pl.semaphore_signal(barrier, inc=1, device_id=device, device_id_type=MESH)
    pl.semaphore_wait(barrier, 65)


def wait_bytes(ref, sem):
    pltpu.make_async_copy(ref, ref, sem).wait()


def step_kernel(
    keys, queries, values, grads, flags,
    attended, q_grad, k_grad, v_grad,
    k, q, v, g, weights, group_grads, outs, dkv, from_side, from_slab, summed, final, kinds, kind,
    send_in, recv_in, halo_send, halo_recv, kind_sems, send_out, recv_out, side_send, side_recv, slab_send, slab_recv
):
    me = spot()
    x, z_hi, core, head, quarter = me["x"], me["z_hi"], me["core"], me["head"], me["quarter"]
    flip = rem(div(head, 2), 2)
    swap = rem(head, 2)

    def row_of(place):
        return place + flip * (2 - 2 * place)

    def part_place(n):
        at = me["sub"] * 3 + n
        tile = core * 12 + div(at, 4)
        column = rem(tile, 8)
        return div(tile, 8), div(column, 2), rem(column, 2), rem(at, 4)

    own_parts = sum((part_place(n)[1] == quarter).astype(jnp.int32) for n in range(3))

    greet(me)

    def send_head(n, target_head, own_head):
        source, out, slab, shift = inputs[n]
        for part_n in range(3):
            row, to, side, part = part_place(part_n)
            first = pl.multiple_of((side + shift) * TILE + part * PART, 16)
            src = source.at[pl.ds(part_n * PART, PART), pl.ds(pl.multiple_of(target_head * DH, DH), DH)]
            dst = out.at[slab, row, pl.ds(first, PART), :]
            remote = copy_to(src, dst, send_in.at[n], recv_in.at[n], worker(x, target_head, to))
            if own_head:

                @pl.when(to == quarter)
                def _():
                    pltpu.make_async_copy(src, dst, recv_in.at[n]).start()

                @pl.when(to != quarter)
                def _():
                    remote.start()

            else:
                remote.start()

    inputs = ((keys, k, 1 + z_hi, 1), (queries, q, z_hi, 0), (values, v, 1 + z_hi, 1), (grads, g, z_hi, 0))

    asker = (
        x * 4 + div(me["sub"], 8) * 2 + core,
        rem(div(me["sub"], 2), 4) * 4 + 2 * rem(me["sub"], 2) + z_hi,
    )
    own_kind = jnp.logical_and(me["sub"] == head, rem(me["y"], 2) == z_hi)

    @pl.when(own_kind)
    def _():
        pltpu.make_async_copy(flags, kinds, kind_sems.at[1]).start()

    @pl.when(jnp.logical_not(own_kind))
    def _():
        copy_to(flags, kinds, kind_sems.at[0], kind_sems.at[1], asker).start()

    for n in range(4):
        pl.loop(1, HEADS)(lambda step: send_head(n, rem(head + step, HEADS), False))
        send_head(n, head, True)

    for a in range(2):
        group_grads[a, 18] = jnp.zeros((SPAN, DH), jnp.float32)

    mine = slice(TILE, TILE + COLS)
    hi, lo = slice(2 * TILE, 3 * TILE), slice(TILE, 2 * TILE)
    top, bottom = slice(3 * TILE, 4 * TILE), slice(0, TILE)
    after = worker(rem(x + 1, 4), head, quarter)
    before = worker(rem(x + 3, 4), head, quarter)

    class Halo:
        def __init__(self, buf, base):
            self.buf, self.base = buf, base
            self.forward = copy_to(
                buf.at[2, :, mine, :], buf.at[0, :, mine, :], halo_send.at[base], halo_recv.at[base], after
            )
            self.backward = copy_to(
                buf.at[1, :, mine, :], buf.at[3, :, mine, :], halo_send.at[base + 1], halo_recv.at[base + 1], before
            )

        def sides(self, n, slabs, action):
            buf, n = self.buf, self.base + n
            to_right, to_left = buf.at[slabs, :, hi, :], buf.at[slabs, :, lo, :]
            at_right, at_left = buf.at[slabs, :, bottom, :], buf.at[slabs, :, top, :]

            def send(j, src, dst, to):
                copy = copy_to(src, dst, halo_send.at[n + j], halo_recv.at[n + j % 2], worker(x, head, to))
                getattr(copy, action)()

            @pl.when(quarter < 3)
            def _():
                send(0, to_right, at_right, rem(quarter + 1, 4))

            @pl.when(quarter > 0)
            def _():
                send(1, to_left, at_left, rem(quarter + 3, 4))

            @pl.when(quarter == 1)
            def _():
                send(2, to_right, at_right, quarter - 1)

            @pl.when(quarter == 2)
            def _():
                send(3, to_left, at_left, quarter + 1)

            if action == "wait_send":
                wait_bytes(at_right, halo_recv.at[n])
                wait_bytes(at_left, halo_recv.at[n + 1])

        def begin(self):
            self.forward.start()
            self.backward.start()
            self.sides(2, slice(1, 3), "start")

        def go_on(self):
            self.forward.wait_recv()
            self.sides(6, 0, "start")
            self.backward.wait_recv()
            self.sides(10, 3, "start")

        def end(self):
            self.sides(2, slice(1, 3), "wait_send")
            self.sides(6, 0, "wait_send")
            self.sides(10, 3, "wait_send")
            self.forward.wait_send()
            self.backward.wait_send()

    key_halo, value_halo = Halo(k, 0), Halo(v, 14)
    wait_bytes(k.at[1:3, :, mine, :], recv_in.at[0])
    key_halo.begin()
    key_halo.go_on()
    wait_bytes(kinds, kind_sems.at[1])
    to_scalar = pltpu.make_async_copy(kinds, kind, kind_sems.at[2])
    to_scalar.start()
    to_scalar.wait()
    along_time = kind[0, 0]
    key_halo.end()
    wait_bytes(q, recv_in.at[1])

    def group_at(n, slab, row):
        return (
            jnp.where(along_time > 0, slab + n, slab + 1),
            jnp.where(along_time > 0, row, jnp.clip(row + n - 1, 0, 2)),
        )

    def places(step):
        return rem(step + swap, 2), row_of(div(step, 2))

    @pl.loop(0, 6)
    def _(step):
        @pl.when(step == 3)
        def _():
            wait_bytes(v.at[1:3, :, mine, :], recv_in.at[2])
            value_halo.begin()

        slab, row = places(step)
        lane = lax.broadcasted_iota(jnp.int32, (1, REACHED), 1)
        for side in range(2):
            rows = q[slab, row, side * TILE : (side + 1) * TILE, :]
            column = 2 * quarter + side
            low = jnp.where(column > 0, 0, TILE)
            high = jnp.where(column < 7, REACHED, 2 * TILE)
            scores = []
            for n in range(3):
                s_at, r_at = group_at(n, slab, row)
                k_rows = k[s_at, r_at, side * TILE : side * TILE + REACHED, :]
                s = lax.dot_general(rows, k_rows, (((1,), (1,)), ((), ())), preferred_element_type=jnp.float32)
                slab_in = 2 * x + slab + n - 1
                ok_time = jnp.logical_and(slab_in >= 0, slab_in < 8).astype(jnp.int32)
                ok_row = jnp.logical_and(row + n - 1 >= 0, row + n - 1 < 3).astype(jnp.int32)
                last = high * jnp.where(along_time > 0, ok_time, ok_row)
                s = s + jnp.where(jnp.logical_and(lane >= low, lane < last), 0.0, NEG_FILL)
                scores.append(s)
            peak = jnp.max(jnp.maximum(jnp.maximum(scores[0], scores[1]), scores[2]), axis=1, keepdims=True)
            raised = [jnp.exp2((s - peak) * (SCALE * LOG2E)) for s in scores]
            share = 1.0 / jnp.sum(raised[0] + raised[1] + raised[2], axis=1, keepdims=True)
            for n in range(3):
                weights[step, side, n] = (raised[n] * share).astype(jnp.bfloat16)

    value_halo.go_on()
    value_halo.end()
    wait_bytes(g, recv_in.at[3])

    def send_part(slab, row, side, part, source, targets, send, recv):
        tile = row * 8 + 2 * quarter + side
        at = rem(tile, 12) * 4 + part
        to_core, sub, n = div(tile, 12), div(at, 3), rem(at, 3)
        ctx = x * 4 + slab * 2 + to_core
        self_part = jnp.logical_and(ctx == lax.axis_index("ctx"), sub == me["sub"])
        first = pl.multiple_of(side * TILE + part * PART, 16)
        for a in range(2):
            src = source.at[a, slab, row, pl.ds(first, PART), :]
            dst = targets[a].at[pl.ds(pl.multiple_of(n * PART, 16), PART), pl.ds(pl.multiple_of(head * DH, DH), DH)]

            @pl.when(self_part)
            def _():
                pltpu.make_async_copy(src, dst, recv).start()

            @pl.when(jnp.logical_not(self_part))
            def _():
                copy_to(src, dst, send, recv, (ctx, sub)).start()

    def side_copies(place):
        row = row_of(place)
        left = worker(x, head, rem(quarter + 3, 4))
        right = worker(x, head, rem(quarter + 1, 4))
        return (
            copy_to(
                dkv.at[:, :, row, top, :], from_side.at[0, :, :, row], side_send.at[0, place], side_recv.at[0, place], right
            ),
            copy_to(
                dkv.at[:, :, row, bottom, :], from_side.at[1, :, :, row], side_send.at[1, place], side_recv.at[1, place], left
            ),
        )

    def gather_groups(place):
        row = row_of(place)
        for s_at in range(4):
            if 1 <= s_at <= 2:
                same = 6 + (s_at - 1) * 3 + row
                previous = jnp.where(
                    along_time > 0,
                    s_at * 3 + row if s_at < 2 else 18,
                    jnp.where(row < 2, (s_at - 1) * 3 + row + 1, 18),
                )
                following = jnp.where(
                    along_time > 0,
                    12 + (s_at - 2) * 3 + row if s_at >= 2 else 18,
                    jnp.where(row > 0, 12 + (s_at - 1) * 3 + row - 1, 18),
                )
                for a in range(2):
                    total = group_grads[a, same] + group_grads[a, previous] + group_grads[a, following]
                    dkv[a, s_at, row] = total.astype(jnp.bfloat16)
            else:
                only = jnp.where(along_time > 0, row if s_at == 0 else 15 + row, 18)
                for a in range(2):
                    dkv[a, s_at, row] = group_grads[a, only].astype(jnp.bfloat16)
        to_right, to_left = side_copies(place)

        @pl.when(quarter < 3)
        def _():
            to_right.start()

        @pl.when(quarter > 0)
        def _():
            to_left.start()

    @pl.loop(0, 6)
    def _(step):
        slab, row = places(step)
        parts = []
        for side in range(2):
            here = slice(side * TILE, (side + 1) * TILE)
            span = slice(side * TILE, side * TILE + REACHED)
            q_rows, g_rows = q[slab, row, here, :], g[slab, row, here, :]
            attend = jnp.zeros((TILE, DH), jnp.float32)
            for n in range(3):
                s_at, r_at = group_at(n, slab, row)
                attend += jnp.dot(weights[step, side, n], v[s_at, r_at, span, :], preferred_element_type=jnp.float32)
            attend = attend.astype(jnp.bfloat16)
            outs[0, slab, row, here, :] = attend
            delta = jnp.sum(g_rows.astype(jnp.float32) * attend.astype(jnp.float32), axis=1, keepdims=True)
            q_sum = jnp.zeros((TILE, DH), jnp.float32)
            for n in range(3):
                s_at, r_at = group_at(n, slab, row)
                w = weights[step, side, n]
                w_grad = lax.dot_general(
                    g_rows, v[s_at, r_at, span, :], (((1,), (1,)), ((), ())), preferred_element_type=jnp.float32
                )
                s_grad = (w.astype(jnp.float32) * (w_grad - delta) * SCALE).astype(jnp.bfloat16)
                q_sum += jnp.dot(s_grad, k[s_at, r_at, span, :], preferred_element_type=jnp.float32)
                block = n * 6 + slab * 3 + row
                for a, left_side, right_side in ((0, s_grad, q_rows), (1, w, g_rows)):
                    piece = lax.dot_general(
                        left_side, right_side, (((0,), (0,)), ((), ())), preferred_element_type=jnp.float32
                    )
                    if side == 0:
                        group_grads[a, block, 0:REACHED] = piece
                    else:
                        group_grads[a, block, TILE:REACHED] += piece[0 : 2 * TILE]
                        group_grads[a, block, REACHED:SPAN] = piece[2 * TILE :]
            outs[1, slab, row, here, :] = q_sum.astype(jnp.bfloat16)

        @pl.loop(0, 8)
        def _(n):
            at = rem(n + 3 * head, 8)
            send_part(slab, row, div(at, 4), rem(at, 4), outs, (attended, q_grad), send_out.at[0], recv_out.at[0])

        @pl.when(step == 3)
        def _():
            gather_groups(0)

    gather_groups(1)
    gather_groups(2)

    def slab_copies(place):
        row = row_of(place)
        return (
            copy_to(summed.at[:, 3, row], from_slab.at[0, :, row], slab_send.at[0, place], slab_recv.at[0, place], after),
            copy_to(summed.at[:, 0, row], from_slab.at[1, :, row], slab_send.at[1, place], slab_recv.at[1, place], before),
        )

    for place in range(3):
        row = row_of(place)
        for side in range(2):
            has = quarter > 0 if side == 0 else quarter < 3
            here = slice((1 + side) * TILE, (2 + side) * TILE)
            there = slice(side * TILE, (1 + side) * TILE)

            @pl.when(has)
            def _():
                wait_bytes(from_side.at[side, :, :, row], side_recv.at[side, place])
                for a in range(2):
                    for s in range(4):
                        summed[a, s, row, there, :] = (
                            dkv[a, s, row, here, :].astype(jnp.float32) + from_side[side, a, s, row].astype(jnp.float32)
                        ).astype(jnp.bfloat16)

            @pl.when(jnp.logical_not(has))
            def _():
                for a in range(2):
                    for s in range(4):
                        summed[a, s, row, there, :] = dkv[a, s, row, here, :]

        to_after, to_before = slab_copies(place)

        @pl.when(x < 3)
        def _():
            to_after.start()

        @pl.when(x > 0)
        def _():
            to_before.start()

    for place in range(3):
        row = row_of(place)
        for slab in range(2):
            has = x > 0 if slab == 0 else x < 3

            @pl.when(has)
            def _():
                wait_bytes(from_slab.at[slab, :, row], slab_recv.at[slab, place])
                for a in range(2):
                    final[a, slab, row] = (
                        summed[a, 1 + slab, row].astype(jnp.float32) + from_slab[slab, a, row].astype(jnp.float32)
                    ).astype(jnp.bfloat16)

            @pl.when(jnp.logical_not(has))
            def _():
                for a in range(2):
                    final[a, slab, row] = summed[a, 1 + slab, row]

        @pl.loop(0, 16)
        def _(n):
            at = rem(n + 3 * head, 16)
            send_part(
                div(at, 8), row, rem(div(at, 4), 2), rem(at, 4), final, (k_grad, v_grad), send_out.at[1], recv_out.at[1]
            )

    for place in range(3):
        to_right, to_left = side_copies(place)
        to_after, to_before = slab_copies(place)
        for has, copy in ((quarter < 3, to_right), (quarter > 0, to_left), (x < 3, to_after), (x > 0, to_before)):

            @pl.when(has)
            def _():
                copy.wait_send()

    for count in range(4):

        @pl.when(own_parts == count)
        def _():
            for n in range(4):
                wait_bytes(k.at[0, :, 0 : SPAN - 16 * count, :], send_in.at[n])
            for n in range(2):
                wait_bytes(dkv.at[:, 0, :, 0 : SPAN - 16 * count, :], send_out.at[n])

    @pl.when(jnp.logical_not(own_kind))
    def _():
        wait_bytes(flags, kind_sems.at[0])

    wait_bytes(outs, recv_out.at[0])
    wait_bytes(final, recv_out.at[1])


def place_kernel(*refs):
    sources, results, buffers, sems = refs[:4], refs[4:8], refs[8:12], refs[12]
    loads = [pltpu.make_async_copy(s, b, sems.at[n]) for n, (s, b) in enumerate(zip(sources, buffers))]
    stores = [pltpu.make_async_copy(b, r, sems.at[4 + n]) for n, (b, r) in enumerate(zip(buffers, results))]
    for c in loads:
        c.start()
    for load, store in zip(loads, stores):
        load.wait()
        store.start()
    for c in stores:
        c.wait()


def per_device(queries, keys, values, out_grad, key_tiles):
    ctx = lax.axis_index("ctx")
    own_slab = ctx // 2
    lists = key_tiles[0]
    along_time = jnp.any(jnp.logical_and(lists >= 0, lists // 24 != own_slab))
    flags = jnp.broadcast_to(along_time.astype(jnp.int32), (8, 128))

    anywhere = pl.BlockSpec(memory_space=pl.ANY)
    token_block = jax.ShapeDtypeStruct((ROWS, HEADS * DH), jnp.bfloat16)
    near = pltpu.VMEM((4, 3, SPAN, DH), jnp.bfloat16)
    own = pltpu.VMEM((2, 3, COLS, DH), jnp.bfloat16)
    pair = pltpu.VMEM((2, 2, 3, COLS, DH), jnp.bfloat16)
    blocks = pl.pallas_call(
        step_kernel,
        name="attention_step",
        out_shape=(token_block,) * 4,
        in_specs=[anywhere] * 5,
        out_specs=(anywhere,) * 4,
        scratch_shapes=[
            near,
            own,
            near,
            own,
            pltpu.VMEM((6, 2, 3, TILE, REACHED), jnp.bfloat16),
            pltpu.VMEM((2, 19, SPAN, DH), jnp.float32),
            pair,
            pltpu.VMEM((2, 4, 3, SPAN, DH), jnp.bfloat16),
            pltpu.VMEM((2, 2, 4, 3, TILE, DH), jnp.bfloat16),
            pair,
            pltpu.VMEM((2, 4, 3, COLS, DH), jnp.bfloat16),
            pair,
            pltpu.VMEM((8, 128), jnp.int32),
            pltpu.SMEM((8, 128), jnp.int32),
            pltpu.SemaphoreType.DMA((4,)),
            pltpu.SemaphoreType.DMA((4,)),
            pltpu.SemaphoreType.DMA((28,)),
            pltpu.SemaphoreType.DMA((28,)),
            pltpu.SemaphoreType.DMA((3,)),
            pltpu.SemaphoreType.DMA((2,)),
            pltpu.SemaphoreType.DMA((2,)),
            pltpu.SemaphoreType.DMA((2, 3)),
            pltpu.SemaphoreType.DMA((2, 3)),
            pltpu.SemaphoreType.DMA((2, 3)),
            pltpu.SemaphoreType.DMA((2, 3)),
        ],
        compiler_params=pltpu.CompilerParams(has_side_effects=True, collective_id=0, vmem_limit_bytes=VMEM_LIMIT),
    )(keys, queries, values, out_grad, flags)
    return pl.pallas_call(
        place_kernel,
        name="place_results",
        out_shape=(token_block,) * 4,
        in_specs=[anywhere] * 4,
        out_specs=(anywhere,) * 4,
        scratch_shapes=[pltpu.VMEM((ROWS, HEADS * DH), jnp.bfloat16)] * 4 + [pltpu.SemaphoreType.DMA((8,))],
        compiler_params=pltpu.CompilerParams(vmem_limit_bytes=VMEM_LIMIT),
    )(*blocks)


def solution(mesh):
    token_spec = P(("ctx", "head"), None)
    return jax.shard_map(
        per_device,
        mesh=mesh,
        in_specs=(token_spec,) * 4 + (P("head", "ctx", None),),
        out_specs=(token_spec,) * 4,
        check_vma=False,
    )
```

time: 786 us -> 136 us (0.17)
  waiting for transfers between devices: 236 us -> 0 us
  blocking collectives: 228 us -> 0 us
  Pallas kernels: 0 us -> 132 us
  local copies, waits for them, and re-layouts: 129 us -> 1.36 us
  other arithmetic: 86.1 us -> 0.65 us
  starting transfers between devices: 78.6 us -> 0 us
  matrix products: 22.1 us -> 0 us
    all_to_all x3 -> x0, blocking collectives: 228 us -> none  [the longest x1 187 us: per_device(): lax.all_to_all(query_grad, 'head', split_axis=0, concat_axis=1, tiled=True)]
    ppermute x12 -> x0, waiting for transfers between devices: 197 us -> none  [shifted(): return lax.ppermute(array, axis, pairs)]
    pallas_call x0 -> x2, Pallas kernels: none -> 132 us  [the longest x1 130 us: per_device(): pl.pallas_call(step_kernel, name='attention_step', out_shape=(token_block...]
    scatter-add x3 -> x0, other arithmetic: 58.2 us -> none  [advance(): grad_store = grad_store.at[chosen.reshape(-1)].add(both_parts)]
    gather x6 -> x0, local copies, waits for them, and re-layouts: 52.5 us -> none  [advance(): gathered = tile_store[chosen]]
    ppermute x12 -> x0, starting transfers between devices: 48.1 us -> none  [shifted(): return lax.ppermute(array, axis, pairs)]
    all_to_all x5 -> x0, waiting for transfers between devices: 39.3 us -> none  [the longest x1 15 us: per_device(): lax.all_to_all(keys, 'head', split_axis=1, concat_axis=0, tiled=True)]
    all_to_all x5 -> x0, starting transfers between devices: 30.5 us -> none  [the longest x1 8.65 us: per_device(): lax.all_to_all(keys, 'head', split_axis=1, concat_axis=0, tiled=True)]
  transfers between devices with their start and end apart: 17 -> 0, of which waited for: 7 -> 0; matrix products, arithmetic and copies ran while one was open for 7% -> 0% of each run, Pallas kernels for 0% -> 0%
where the time goes in v3:
time: 136 us
  Pallas kernels  132 us (97%)
  local copies, waits for them, and re-layouts  1.36 us (1%)
    pallas_call x1, Pallas kernels, per_device(): pl.pallas_call(step_kernel, name='attention_step', out_shape=(token_block...  130 us

profile of v3, /device:TPU:34, one launch (start us, length us, event | category | flops | bytes accessed | tf_op | source)
XLA Modules:
  0.0 135.7 jit_solution(9161137901393347286)
XLA Ops:
  0.6 0.0 copy-start
  0.7 0.7 copy-done
  1.3 0.1 copy.9
  1.4 0.6 fusion.3
  2.7 0.6 broadcast_in_dim.3.flags
  3.3 129.9 %attention_step.1 = (bf16[144,2048]{1,0:T(8,128)(2,1)}, bf16[144,2048]{1,0:T(8,128)(2,1)}, bf16[144,2048]{1,0:T(8,128)(2,1)}, bf16[144,2048]{1,0:T(8,128)(2,1)}) custom-call(bf16[144,2048]{1,0:T(8,128)(2,1)} %keys.1, bf16[144,2048]{1,0:T(8,128)(2,1)} %queries.1, bf16[144,2048]{1,0:T(8,128)(2,1)} %values.1, bf16[144,2048]{1,0:T(8,128)(2,1)} %grads.1, ...), custom_call_target="tpu_custom_call" | custom-call | tf_op jit(solution)/shard_map/attention_step/pallas_call | solution.py:491
  133.2 2.5 %place_results.1 = (bf16[144,2048]{1,0:T(8,128)(2,1)}, bf16[144,2048]{1,0:T(8,128)(2,1)}, bf16[144,2048]{1,0:T(8,128)(2,1)}, bf16[144,2048]{1,0:T(8,128)(2,1)}) custom-call(bf16[144,2048]{1,0:T(8,128)(2,1)} %get-tuple-element.8.refs_0_, bf16[144,2048]{1,0:T(8,128)(2,1)} %get-tuple-element.9.refs_1_, bf16[144,2048]{1,0:T(8,128)(2,1)} %get-tuple-element.10.refs_2_, ...), custom_call_target="tpu_custom_call" | custom-call | tf_op jit(solution)/shard_map/place_results/pallas_call | solution.py:526
Async XLA Ops:
  0.6 0.7 copy-start

commit v4 on v3

--- a/solution.py
+++ b/solution.py
@@ -325,10 +325,73 @@
         def _():
             to_left.start()
 
+    def slab_copies(place):
+        row = row_of(place)
+        return (
+            copy_to(summed.at[:, 3, row], from_slab.at[0, :, row], slab_send.at[0, place], slab_recv.at[0, place], after),
+            copy_to(summed.at[:, 0, row], from_slab.at[1, :, row], slab_send.at[1, place], slab_recv.at[1, place], before),
+        )
+
+    def add_sides(place):
+        row = row_of(place)
+        for side in range(2):
+            has = quarter > 0 if side == 0 else quarter < 3
+            here = slice((1 + side) * TILE, (2 + side) * TILE)
+            there = slice(side * TILE, (1 + side) * TILE)
+
+            @pl.when(has)
+            def _():
+                wait_bytes(from_side.at[side, :, :, row], side_recv.at[side, place])
+                for a in range(2):
+                    for s in range(4):
+                        summed[a, s, row, there, :] = (
+                            dkv[a, s, row, here, :].astype(jnp.float32) + from_side[side, a, s, row].astype(jnp.float32)
+                        ).astype(jnp.bfloat16)
+
+            @pl.when(jnp.logical_not(has))
+            def _():
+                for a in range(2):
+                    for s in range(4):
+                        summed[a, s, row, there, :] = dkv[a, s, row, here, :]
+
+        to_after, to_before = slab_copies(place)
+
+        @pl.when(x < 3)
+        def _():
+            to_after.start()
+
+        @pl.when(x > 0)
+        def _():
+            to_before.start()
+
+    def finish(place):
+        row = row_of(place)
+        for slab in range(2):
+            has = x > 0 if slab == 0 else x < 3
+
+            @pl.when(has)
+            def _():
+                wait_bytes(from_slab.at[slab, :, row], slab_recv.at[slab, place])
+                for a in range(2):
+                    final[a, slab, row] = (
+                        summed[a, 1 + slab, row].astype(jnp.float32) + from_slab[slab, a, row].astype(jnp.float32)
+                    ).astype(jnp.bfloat16)
+
+            @pl.when(jnp.logical_not(has))
+            def _():
+                for a in range(2):
+                    final[a, slab, row] = summed[a, 1 + slab, row]
+
+        @pl.loop(0, 16)
+        def _(n):
+            at = rem(n + 3 * head, 16)
+            send_part(
+                div(at, 8), row, rem(div(at, 4), 2), rem(at, 4), final, (k_grad, v_grad), send_out.at[1], recv_out.at[1]
+            )
+
     @pl.loop(0, 6)
     def _(step):
         slab, row = places(step)
-        parts = []
         for side in range(2):
             here = slice(side * TILE, (side + 1) * TILE)
             span = slice(side * TILE, side * TILE + REACHED)
@@ -361,81 +424,26 @@
                         group_grads[a, block, REACHED:SPAN] = piece[2 * TILE :]
             outs[1, slab, row, here, :] = q_sum.astype(jnp.bfloat16)
 
+        @pl.when(step == 3)
+        def _():
+            gather_groups(0)
+
+        @pl.when(step == 5)
+        def _():
+            gather_groups(1)
+            add_sides(0)
+            gather_groups(2)
+
         @pl.loop(0, 8)
         def _(n):
             at = rem(n + 3 * head, 8)
             send_part(slab, row, div(at, 4), rem(at, 4), outs, (attended, q_grad), send_out.at[0], recv_out.at[0])
 
-        @pl.when(step == 3)
-        def _():
-            gather_groups(0)
-
-    gather_groups(1)
-    gather_groups(2)
-
-    def slab_copies(place):
-        row = row_of(place)
-        return (
-            copy_to(summed.at[:, 3, row], from_slab.at[0, :, row], slab_send.at[0, place], slab_recv.at[0, place], after),
-            copy_to(summed.at[:, 0, row], from_slab.at[1, :, row], slab_send.at[1, place], slab_recv.at[1, place], before),
-        )
-
-    for place in range(3):
-        row = row_of(place)
-        for side in range(2):
-            has = quarter > 0 if side == 0 else quarter < 3
-            here = slice((1 + side) * TILE, (2 + side) * TILE)
-            there = slice(side * TILE, (1 + side) * TILE)
-
-            @pl.when(has)
-            def _():
-                wait_bytes(from_side.at[side, :, :, row], side_recv.at[side, place])
-                for a in range(2):
-                    for s in range(4):
-                        summed[a, s, row, there, :] = (
-                            dkv[a, s, row, here, :].astype(jnp.float32) + from_side[side, a, s, row].astype(jnp.float32)
-                        ).astype(jnp.bfloat16)
-
-            @pl.when(jnp.logical_not(has))
-            def _():
-                for a in range(2):
-                    for s in range(4):
-                        summed[a, s, row, there, :] = dkv[a, s, row, here, :]
-
-        to_after, to_before = slab_copies(place)
-
-        @pl.when(x < 3)
-        def _():
-            to_after.start()
-
-        @pl.when(x > 0)
-        def _():
-            to_before.start()
-
-    for place in range(3):
-        row = row_of(place)
-        for slab in range(2):
-            has = x > 0 if slab == 0 else x < 3
-
-            @pl.when(has)
-            def _():
-                wait_bytes(from_slab.at[slab, :, row], slab_recv.at[slab, place])
-                for a in range(2):
-                    final[a, slab, row] = (
-                        summed[a, 1 + slab, row].astype(jnp.float32) + from_slab[slab, a, row].astype(jnp.float32)
-                    ).astype(jnp.bfloat16)
-
-            @pl.when(jnp.logical_not(has))
-            def _():
-                for a in range(2):
-                    final[a, slab, row] = summed[a, 1 + slab, row]
-
-        @pl.loop(0, 16)
-        def _(n):
-            at = rem(n + 3 * head, 16)
-            send_part(
-                div(at, 8), row, rem(div(at, 4), 2), rem(at, 4), final, (k_grad, v_grad), send_out.at[1], recv_out.at[1]
-            )
+    add_sides(1)
+    finish(0)
+    add_sides(2)
+    finish(1)
+    finish(2)
 
     for place in range(3):
         to_right, to_left = side_copies(place)

time: 136 us -> 137 us (level)
  no operation moved by 1% of the time
where the time goes in v4:
time: 137 us
  Pallas kernels  133 us (97%)
    pallas_call x1, Pallas kernels, per_device(): pl.pallas_call(step_kernel, name='attention_step', out_shape=(token_block...  131 us

profile of v4, /device:TPU:34, one launch (start us, length us, event | category | flops | bytes accessed | tf_op | source)
XLA Modules:
  0.0 136.5 jit_solution(2166648498558354328)
XLA Ops:
  0.6 0.0 copy-start
  0.7 0.7 copy-done
  1.3 0.1 copy.9
  1.4 0.6 fusion.3
  2.7 0.6 broadcast_in_dim.3.flags
  3.3 130.7 %attention_step.1 = (bf16[144,2048]{1,0:T(8,128)(2,1)}, bf16[144,2048]{1,0:T(8,128)(2,1)}, bf16[144,2048]{1,0:T(8,128)(2,1)}, bf16[144,2048]{1,0:T(8,128)(2,1)}) custom-call(bf16[144,2048]{1,0:T(8,128)(2,1)} %keys.1, bf16[144,2048]{1,0:T(8,128)(2,1)} %queries.1, bf16[144,2048]{1,0:T(8,128)(2,1)} %values.1, bf16[144,2048]{1,0:T(8,128)(2,1)} %grads.1, ...), custom_call_target="tpu_custom_call" | custom-call | tf_op jit(solution)/shard_map/attention_step/pallas_call | solution.py:499
  134.0 2.5 %place_results.1 = (bf16[144,2048]{1,0:T(8,128)(2,1)}, bf16[144,2048]{1,0:T(8,128)(2,1)}, bf16[144,2048]{1,0:T(8,128)(2,1)}, bf16[144,2048]{1,0:T(8,128)(2,1)}) custom-call(bf16[144,2048]{1,0:T(8,128)(2,1)} %get-tuple-element.8.refs_0_, bf16[144,2048]{1,0:T(8,128)(2,1)} %get-tuple-element.9.refs_1_, bf16[144,2048]{1,0:T(8,128)(2,1)} %get-tuple-element.10.refs_2_, ...), custom_call_target="tpu_custom_call" | custom-call | tf_op jit(solution)/shard_map/place_results/pallas_call | solution.py:534
Async XLA Ops:
  0.6 0.7 copy-start

commit v5 on v3

--- a/solution.py
+++ b/solution.py
@@ -259,16 +259,15 @@
 
     value_halo.go_on()
     value_halo.end()
-    wait_bytes(g, recv_in.at[3])
-
-    def send_part(slab, row, side, part, source, targets, send, recv):
+
+    def send_part(slab, row, side, part, arrays, source, targets, send, recv):
         tile = row * 8 + 2 * quarter + side
         at = rem(tile, 12) * 4 + part
         to_core, sub, n = div(tile, 12), div(at, 3), rem(at, 3)
         ctx = x * 4 + slab * 2 + to_core
         self_part = jnp.logical_and(ctx == lax.axis_index("ctx"), sub == me["sub"])
         first = pl.multiple_of(side * TILE + part * PART, 16)
-        for a in range(2):
+        for a in arrays:
             src = source.at[a, slab, row, pl.ds(first, PART), :]
             dst = targets[a].at[pl.ds(pl.multiple_of(n * PART, 16), PART), pl.ds(pl.multiple_of(head * DH, DH), DH)]
 
@@ -279,6 +278,26 @@
             @pl.when(jnp.logical_not(self_part))
             def _():
                 copy_to(src, dst, send, recv, (ctx, sub)).start()
+
+    def send_out_part(slab, row, at, a):
+        send_part(slab, row, div(at, 4), rem(at, 4), (a,), outs, (attended, q_grad), send_out.at[0], recv_out.at[0])
+
+    @pl.loop(0, 6)
+    def _(step):
+        slab, row = places(step)
+        for side in range(2):
+            span = slice(side * TILE, side * TILE + REACHED)
+            attend = jnp.zeros((TILE, DH), jnp.float32)
+            for n in range(3):
+                s_at, r_at = group_at(n, slab, row)
+                attend += jnp.dot(weights[step, side, n], v[s_at, r_at, span, :], preferred_element_type=jnp.float32)
+            outs[0, slab, row, side * TILE : (side + 1) * TILE, :] = attend.astype(jnp.bfloat16)
+
+        @pl.loop(0, 8)
+        def _(n):
+            send_out_part(slab, row, rem(n + 3 * head, 8), 0)
+
+    wait_bytes(g, recv_in.at[3])
 
     def side_copies(place):
         row = row_of(place)
@@ -328,17 +347,11 @@
     @pl.loop(0, 6)
     def _(step):
         slab, row = places(step)
-        parts = []
         for side in range(2):
             here = slice(side * TILE, (side + 1) * TILE)
             span = slice(side * TILE, side * TILE + REACHED)
             q_rows, g_rows = q[slab, row, here, :], g[slab, row, here, :]
-            attend = jnp.zeros((TILE, DH), jnp.float32)
-            for n in range(3):
-                s_at, r_at = group_at(n, slab, row)
-                attend += jnp.dot(weights[step, side, n], v[s_at, r_at, span, :], preferred_element_type=jnp.float32)
-            attend = attend.astype(jnp.bfloat16)
-            outs[0, slab, row, here, :] = attend
+            attend = outs[0, slab, row, here, :]
             delta = jnp.sum(g_rows.astype(jnp.float32) * attend.astype(jnp.float32), axis=1, keepdims=True)
             q_sum = jnp.zeros((TILE, DH), jnp.float32)
             for n in range(3):
@@ -364,7 +377,7 @@
         @pl.loop(0, 8)
         def _(n):
             at = rem(n + 3 * head, 8)
-            send_part(slab, row, div(at, 4), rem(at, 4), outs, (attended, q_grad), send_out.at[0], recv_out.at[0])
+            send_out_part(slab, row, at, 1)
 
         @pl.when(step == 3)
         def _():
@@ -434,7 +447,7 @@
         def _(n):
             at = rem(n + 3 * head, 16)
             send_part(
-                div(at, 8), row, rem(div(at, 4), 2), rem(at, 4), final, (k_grad, v_grad), send_out.at[1], recv_out.at[1]
+                div(at, 8), row, rem(div(at, 4), 2), rem(at, 4), (0, 1), final, (k_grad, v_grad), send_out.at[1], recv_out.at[1]
             )
 
     for place in range(3):

time: 136 us -> 135 us (level); the launches traced: 136 us -> 133 us
  Pallas kernels: 132 us -> 129 us
    pallas_call x1, Pallas kernels: 130 us -> 127 us  [per_device(): pl.pallas_call(step_kernel, name='attention_step', out_shape=(token_block...]
where the time goes in v5:
time: 135 us; the launch traced here: 133 us
  Pallas kernels  129 us (96%)
  local copies, waits for them, and re-layouts  1.36 us (1%)
    pallas_call x1, Pallas kernels, per_device(): pl.pallas_call(step_kernel, name='attention_step', out_shape=(token_block...  127 us

profile of v5, /device:TPU:34, one launch (start us, length us, event | category | flops | bytes accessed | tf_op | source)
XLA Modules:
  0.0 132.6 jit_solution(6421456818733601527)
XLA Ops:
  0.6 0.0 copy-start
  0.7 0.7 copy-done
  1.3 0.1 copy.9
  1.4 0.6 fusion.3
  2.7 0.6 broadcast_in_dim.3.flags
  3.3 126.8 %attention_step.1 = (bf16[144,2048]{1,0:T(8,128)(2,1)}, bf16[144,2048]{1,0:T(8,128)(2,1)}, bf16[144,2048]{1,0:T(8,128)(2,1)}, bf16[144,2048]{1,0:T(8,128)(2,1)}) custom-call(bf16[144,2048]{1,0:T(8,128)(2,1)} %keys.1, bf16[144,2048]{1,0:T(8,128)(2,1)} %queries.1, bf16[144,2048]{1,0:T(8,128)(2,1)} %values.1, bf16[144,2048]{1,0:T(8,128)(2,1)} %grads.1, ...), custom_call_target="tpu_custom_call" | custom-call | tf_op jit(solution)/shard_map/attention_step/pallas_call | solution.py:504
  130.1 2.5 %place_results.1 = (bf16[144,2048]{1,0:T(8,128)(2,1)}, bf16[144,2048]{1,0:T(8,128)(2,1)}, bf16[144,2048]{1,0:T(8,128)(2,1)}, bf16[144,2048]{1,0:T(8,128)(2,1)}) custom-call(bf16[144,2048]{1,0:T(8,128)(2,1)} %get-tuple-element.8.refs_0_, bf16[144,2048]{1,0:T(8,128)(2,1)} %get-tuple-element.9.refs_1_, bf16[144,2048]{1,0:T(8,128)(2,1)} %get-tuple-element.10.refs_2_, ...), custom_call_target="tpu_custom_call" | custom-call | tf_op jit(solution)/shard_map/place_results/pallas_call | solution.py:539
Async XLA Ops:
  0.6 0.7 copy-start
